TPU v7x, 32 devices: a whole 2x2x4 slice. The times are simulated.
32 devices in a mesh: row: 4 (over z), col: 8 (over y, x, core).
Axes of the slice: x: 2, y: 2, z: 4, core: 2. Of those that a mesh axis runs over, the one named last changes fastest.
Arguments:
- tokens: bfloat16 [2, 96, 128, 512], P(None, 'row', 'col'), may hold values from -6 to 6
- w_qkv: bfloat16 [512, 1536], replicated, may hold values from -0.25 to 0.25
- w_out: bfloat16 [512, 512], replicated, may hold values from -0.25 to 0.25
- q_saved: bfloat16 [2, 96, 128, 512], P(None, 'row', 'col'), may hold values from -4 to 4
- k_saved: bfloat16 [2, 96, 128, 512], P(None, 'row', 'col'), may hold values from -4 to 4
- v_saved: bfloat16 [2, 96, 128, 512], P(None, 'row', 'col'), may hold values from -4 to 4
- scale_exp: int32 [2, 12, 16, 24], P(None, 'row', 'col'), may hold values from -1 to 1
- grad_out: bfloat16 [2, 96, 128, 512], P(None, 'row', 'col'), may hold values from -6 to 6
- crop_start: int32 [2, 2], replicated, may hold values from 0 to 3
Outputs:
- grad_tokens: bfloat16 [2, 96, 128, 512], P(None, 'row', 'col')
- grad_w_qkv: float32 [512, 1536], P('row', 'col')
- grad_w_out: float32 [512, 512], P('row', 'col')
Inputs may be any that keep to these rules, and one draw needn't show every extreme that they name: crop_start[b] holds the first row and the first column of the region of frame b that the loss covers.
All inputs are finite; a program needn't handle non-finite values.
Results may differ from a plain program's by a relative error of at most 0.017.
Values may be sent and summed in bfloat16 or wider, within the bound.
A program may use at most 128 MiB of HBM per device.

v0:
```python
import math

import jax
import jax.numpy as jnp
from jax import lax
from jax.sharding import PartitionSpec as P

HEADS = 8
RADIUS = 4
BLOCK = 8


max_norm = 1000.0
masked_score = -1e30
tiny_square = 1e-06


def passed_along(array, axis, by):
    size = lax.axis_size(axis)
    pairs = [(i, i + by) for i in range(size) if 0 <= i + by < size]
    return lax.ppermute(array, axis, pairs)


def padded_2(cells, sides, width):
    for axis, dim in sides:
        count = lax.axis_size(axis)
        ends = count - 1
        head = lax.slice_in_dim(cells, 0, width, axis=dim)
        tail = lax.slice_in_dim(cells, cells.shape[dim] - width, cells.shape[dim], axis=dim)
        cells = jnp.concatenate(
            [
                lax.ppermute(tail, axis, [(i, (i + 1) % count) for i in range(ends)]),
                cells,
                lax.ppermute(head, axis, [((i + 1) % count, i) for i in range(ends)]),
            ],
            axis=dim,
        )
    return cells


def product(form, left, right):
    return jnp.einsum(form, left, right, preferred_element_type=jnp.float32)


def dequantize(mantissa, exponent):
    members, height, breadth, features = mantissa.shape
    heads = exponent.shape[3]
    factor = jnp.exp2(exponent.astype(jnp.float32))
    factor = jnp.repeat(jnp.repeat(factor, BLOCK, axis=1), BLOCK, axis=2)
    scaled = (
        mantissa.astype(jnp.float32).reshape(members, height, breadth, heads, features // heads)
        * factor[..., None]
    )
    return scaled.reshape(members, height, breadth, features).astype(jnp.bfloat16)


def query_tiles(tensor):
    height, breadth, features = tensor.shape
    blocked = tensor.reshape(
        height // BLOCK, BLOCK, breadth // BLOCK, BLOCK, HEADS, features // HEADS
    )
    return blocked.transpose(0, 2, 1, 3, 4, 5).reshape(
        height // BLOCK, breadth // BLOCK, BLOCK * BLOCK, HEADS, features // HEADS
    )


def query_untile(tile_set, height, breadth):
    tile_rows, tile_cols = (tile_set.shape[0], tile_set.shape[1])
    features = tile_set.shape[3] * tile_set.shape[4]
    blocked = tile_set.reshape(tile_rows, tile_cols, BLOCK, BLOCK, features)
    return blocked.transpose(0, 2, 1, 3, 4).reshape(height, breadth, features)


def key_tiles(padded):
    height, breadth, features = padded.shape
    tile_rows = height // BLOCK - 1
    tile_cols = breadth // BLOCK - 1
    blocked = padded.reshape(tile_rows + 1, BLOCK, tile_cols + 1, BLOCK, features)
    paired = jnp.stack([blocked[:-1], blocked[1:]], axis=1).reshape(
        tile_rows, 2 * BLOCK, tile_cols + 1, BLOCK, features
    )
    paired = jnp.stack([paired[:, :, :-1], paired[:, :, 1:]], axis=3).reshape(
        tile_rows, 2 * BLOCK, tile_cols, 2 * BLOCK, features
    )
    return paired.transpose(0, 2, 1, 3, 4).reshape(
        tile_rows, tile_cols, 4 * BLOCK * BLOCK, HEADS, features // HEADS
    )


def fold_keys(tile_set):
    tile_rows, tile_cols = (tile_set.shape[0], tile_set.shape[1])
    features = tile_set.shape[3] * tile_set.shape[4]
    tile_grid = tile_set.reshape(tile_rows, tile_cols, 2, BLOCK, 2, BLOCK, features).transpose(
        0, 2, 3, 1, 4, 5, 6
    )
    zero_row = jnp.zeros((1, BLOCK, tile_cols, 2, BLOCK, features), tile_set.dtype)
    summed = jnp.concatenate([tile_grid[:, 0], zero_row], 0) + jnp.concatenate(
        [zero_row, tile_grid[:, 1]], 0
    )
    zero_col = jnp.zeros((tile_rows + 1, BLOCK, 1, BLOCK, features), tile_set.dtype)
    summed = jnp.concatenate([summed[:, :, :, 0], zero_col], 2) + jnp.concatenate(
        [zero_col, summed[:, :, :, 1]], 2
    )
    return summed.reshape((tile_rows + 1) * BLOCK, (tile_cols + 1) * BLOCK, features)


def key_valid(anchor, tile_count, extent):
    position = (
        anchor
        + BLOCK * jnp.arange(tile_count, dtype=jnp.int32)[:, None]
        + jnp.arange(2 * BLOCK, dtype=jnp.int32)[None, :]
    )
    return (position >= 0) & (position < extent)


def window_mask():
    reach = (
        jnp.arange(2 * BLOCK, dtype=jnp.int32)[None, :]
        - jnp.arange(BLOCK, dtype=jnp.int32)[:, None]
    )
    inside = (reach >= 0) & (reach <= 2 * RADIUS)
    return (inside[:, None, :, None] & inside[None, :, None, :]).reshape(
        BLOCK * BLOCK, 4 * BLOCK * BLOCK
    )


def attend(
    queries, grads_attn, keys_pad, values_pad, row_anchor, col_anchor, frame_rows, frame_cols
):
    height, breadth, features = queries.shape
    score_scale = 1.0 / math.sqrt(features // HEADS)
    q_tiles = query_tiles(queries)
    g_tiles = query_tiles(grads_attn)
    k_tiles = key_tiles(keys_pad)
    v_tiles = key_tiles(values_pad)
    tile_rows, tile_cols = (q_tiles.shape[0], q_tiles.shape[1])
    row_ok = key_valid(row_anchor, tile_rows, frame_rows)
    col_ok = key_valid(col_anchor, tile_cols, frame_cols)
    keys_ok = (row_ok[:, None, :, None] & col_ok[None, :, None, :]).reshape(
        tile_rows, tile_cols, 1, 1, 4 * BLOCK * BLOCK
    )
    allowed = keys_ok & window_mask()[None, None, None]
    scores = product("ijqhd,ijkhd->ijhqk", q_tiles, k_tiles) * score_scale
    scores = jnp.where(allowed, scores, masked_score)
    row_max = jnp.max(scores, axis=-1, keepdims=True)
    weights = jnp.exp(scores - row_max)
    softmax = weights / jnp.sum(weights, axis=-1, keepdims=True)
    softmax_half = softmax.astype(jnp.bfloat16)
    out_tiles = product("ijhqk,ijkhd->ijqhd", softmax_half, v_tiles).astype(jnp.bfloat16)
    row_delta = product("ijqhd,ijqhd->ijhq", g_tiles, out_tiles)
    grad_probs = product("ijqhd,ijkhd->ijhqk", g_tiles, v_tiles)
    grad_scores = (softmax * (grad_probs - row_delta[..., None]) * score_scale).astype(jnp.bfloat16)
    grad_q_tiles = product("ijhqk,ijkhd->ijqhd", grad_scores, k_tiles)
    grad_k_tiles = product("ijhqk,ijqhd->ijkhd", grad_scores, q_tiles)
    grad_v_tiles = product("ijhqk,ijqhd->ijkhd", softmax_half, g_tiles)
    return (
        query_untile(out_tiles, height, breadth),
        query_untile(grad_q_tiles, height, breadth),
        fold_keys(grad_k_tiles),
        fold_keys(grad_v_tiles),
    )


def return_rims(padded_grads):
    interior = padded_grads[:, :, :, RADIUS:-RADIUS]
    for offset in (1, -1):
        border_part = (
            padded_grads[:, :, :, -RADIUS:] if offset == 1 else padded_grads[:, :, :, :RADIUS]
        )
        arrived = passed_along(border_part, "col", offset)
        if offset == 1:
            interior = interior.at[:, :, :, :RADIUS].add(arrived)
        else:
            interior = interior.at[:, :, :, -RADIUS:].add(arrived)
    owned = interior[:, :, RADIUS:-RADIUS]
    for offset in (1, -1):
        border_part = interior[:, :, -RADIUS:] if offset == 1 else interior[:, :, :RADIUS]
        arrived = passed_along(border_part, "row", offset)
        if offset == 1:
            owned = owned.at[:, :, :RADIUS].add(arrived)
        else:
            owned = owned.at[:, :, -RADIUS:].add(arrived)
    return owned


def body(tokens, w_qkv, w_out, q_saved, k_saved, v_saved, scale_exp, grad_out, crop_start):
    members, height, breadth, features = tokens.shape
    queries = dequantize(q_saved, scale_exp[..., :HEADS])
    keys_full = dequantize(k_saved, scale_exp[..., HEADS : 2 * HEADS])
    values = dequantize(v_saved, scale_exp[..., 2 * HEADS :])
    row_index = lax.axis_index("row")
    col_index = lax.axis_index("col")
    frame_rows = height * lax.axis_size("row")
    frame_cols = breadth * lax.axis_size("col")
    row_place = row_index * height + jnp.arange(height, dtype=jnp.int32)
    col_place = col_index * breadth + jnp.arange(breadth, dtype=jnp.int32)
    inside = (row_place[None, :, None] >= crop_start[:, 0][:, None, None]) & (
        col_place[None, None, :] >= crop_start[:, 1][:, None, None]
    )
    masked = jnp.where(inside[..., None], grad_out, jnp.zeros_like(grad_out))
    flat_grad = masked.reshape(-1, features)
    grad_attn = lax.dot_general(
        flat_grad, w_out, (((1,), (1,)), ((), ())), preferred_element_type=jnp.float32
    )
    grad_attn = grad_attn.astype(jnp.bfloat16).reshape(masked.shape)
    stacked = jnp.stack([keys_full, values])
    padded = padded_2(stacked, (("row", 2), ("col", 3)), RADIUS)

    def one_member(member):
        q_member, g_member, k_member, v_member = member
        return attend(
            q_member,
            g_member,
            k_member,
            v_member,
            row_index * height - RADIUS,
            col_index * breadth - RADIUS,
            frame_rows,
            frame_cols,
        )

    attn_out, grad_query, grad_k_pad, grad_v_pad = lax.map(
        one_member, (queries, grad_attn, padded[0], padded[1])
    )
    owned = return_rims(jnp.stack([grad_k_pad, grad_v_pad]))
    grad_key, grad_value = (owned[0], owned[1])
    flat_qkv = (
        jnp.concatenate([grad_query, grad_key, grad_value], axis=-1)
        .astype(jnp.bfloat16)
        .reshape(-1, 3 * features)
    )
    grad_tokens = lax.dot_general(
        flat_qkv, w_qkv, (((1,), (1,)), ((), ())), preferred_element_type=jnp.float32
    )
    grad_tokens = grad_tokens.astype(jnp.bfloat16).reshape(tokens.shape)
    raw_qkv = lax.dot_general(
        tokens.reshape(-1, features),
        flat_qkv,
        (((0,), (0,)), ((), ())),
        preferred_element_type=jnp.float32,
    )
    raw_out = lax.dot_general(
        attn_out.reshape(-1, features),
        flat_grad,
        (((0,), (0,)), ((), ())),
        preferred_element_type=jnp.float32,
    )
    whole_qkv, whole_out = lax.psum((raw_qkv, raw_out), ("row", "col"))
    squares = jnp.sum(whole_qkv * whole_qkv) + jnp.sum(whole_out * whole_out)
    rows_each = features // lax.axis_size("row")
    qkv_cols = 3 * features // lax.axis_size("col")
    out_cols = features // lax.axis_size("col")
    part_qkv = lax.dynamic_slice(
        whole_qkv, (row_index * rows_each, col_index * qkv_cols), (rows_each, qkv_cols)
    )
    part_out = lax.dynamic_slice(
        whole_out, (row_index * rows_each, col_index * out_cols), (rows_each, out_cols)
    )
    factor = jnp.minimum(1.0, max_norm / jnp.sqrt(squares + tiny_square))
    return (grad_tokens, factor * part_qkv, factor * part_out)


def solution(mesh):
    placed = (
        P(None, "row", "col", None),
        P(),
        P(),
        P(None, "row", "col", None),
        P(None, "row", "col", None),
        P(None, "row", "col", None),
        P(None, "row", "col", None),
        P(None, "row", "col", None),
        P(),
    )
    return jax.shard_map(
        body,
        mesh=mesh,
        in_specs=placed,
        out_specs=(P(None, "row", "col", None), P("row", "col"), P("row", "col")),
        check_vma=False,
    )
```

profile of v0, /device:TPU:0, one launch (start us, length us, event | category | flops | bytes accessed | tf_op | source)
XLA Modules:
  0.0 465.0 jit_solution(9168266061171627752)
XLA Ops:
  10.3 3.8 mul.121
  16.3 3.7 mul.125
  25.1 6.3 %collective-permute-start = (bf16[2,2,4,16,512]{4,3,2,1,0:T(8,128)(2,1)}, bf16[2,2,4,16,512]{4,3,2,1,0:T(8,128)(2,1)}, u32[]{:S(2)}, u32[]{:S(2)}) collective-permute-start(bf16[2,2,4,16,512]{4,3,2,1,0:T(8,128)(2,1)} %get-tuple-element.293), channel_id=1, source_target_pairs={{0,8},{8,16},{16,24},{1,9},{9,17},{17,25},{2,10},{10,18},{18,26},{... | collective-permute-start | bytes 786440 | tf_op jit(solution)/shard_map/ppermute | solution.py:32
  33.6 3.8 mul.131
  48.1 3.2 pad_maximum_fusion.4
  53.1 190.3 %while.24 = (s32[]{:T(128)}, bf16[2,24,16,512]{3,2,1,0:T(8,128)(2,1)}, bf16[2,24,16,512]{3,1,2,0:T(8,128)(2,1)}, f32[2,32,24,512]{3,1,2,0:T(8,128)}, f32[2,32,24...) while((s32[]{:T(128)}, ...), condition=%wide.region_3.4_spmd.clone, body=%wide.region_0.3_spmd.sunk.clone | while | flops 621461056 | bytes 255329296 | solution.py:222
  63.5 4.5 copy.194
  71.7 3.4 copy.196
  77.5 3.3 fusion.117
  81.8 4.4 fusion.120
  93.8 3.5 multiply_convert_fusion.6
  103.0 4.4 convolution_bitcast_fusion.12
  107.4 5.9 %copy.201 = f32[3,2,256,8,64]{4,3,2,1,0:T(8,128)} copy(f32[3,2,256,8,64]{2,4,3,1,0:T(8,128)} %convolution_bitcast_fusion.12) | data formatting | bytes 6291456 | tf_op jit(solution)/shard_map/while/body/eval_jaxpr/ijhqk,ijqhd->ijkhd/transpose | solution.py:42
  113.3 6.2 %reshape.552 = f32[3,2,2,8,2,8,512]{6,5,4,3,2,1,0:T(8,128)} reshape(f32[3,2,256,8,64]{4,3,2,1,0:T(8,128)} %copy.201) | data formatting | bytes 6291456 | tf_op jit(solution)/shard_map/while/body/eval_jaxpr/reshape | solution.py:93
  126.0 5.9 %copy.203 = f32[3,2,256,8,64]{4,3,2,1,0:T(8,128)} copy(f32[3,2,256,8,64]{2,4,3,1,0:T(8,128)} %convolution_bitcast_fusion.13) | data formatting | bytes 6291456 | tf_op jit(solution)/shard_map/while/body/eval_jaxpr/ijhqk,ijqhd->ijkhd/transpose | solution.py:42
  131.8 6.2 %reshape.553 = f32[3,2,2,8,2,8,512]{6,5,4,3,2,1,0:T(8,128)} reshape(f32[3,2,256,8,64]{4,3,2,1,0:T(8,128)} %copy.203) | data formatting | bytes 6291456 | tf_op jit(solution)/shard_map/while/body/eval_jaxpr/reshape | solution.py:93
  158.6 4.5 copy.194
  166.9 3.4 copy.196
  172.7 3.3 fusion.117
  177.0 4.4 fusion.120
  188.9 3.5 multiply_convert_fusion.6
  198.1 4.4 convolution_bitcast_fusion.12
  202.6 5.9 %copy.201 = f32[3,2,256,8,64]{4,3,2,1,0:T(8,128)} copy(f32[3,2,256,8,64]{2,4,3,1,0:T(8,128)} %convolution_bitcast_fusion.12) | data formatting | bytes 6291456 | tf_op jit(solution)/shard_map/while/body/eval_jaxpr/ijhqk,ijqhd->ijkhd/transpose | solution.py:42
  208.5 6.2 %reshape.552 = f32[3,2,2,8,2,8,512]{6,5,4,3,2,1,0:T(8,128)} reshape(f32[3,2,256,8,64]{4,3,2,1,0:T(8,128)} %copy.201) | data formatting | bytes 6291456 | tf_op jit(solution)/shard_map/while/body/eval_jaxpr/reshape | solution.py:93
  221.2 5.9 %copy.203 = f32[3,2,256,8,64]{4,3,2,1,0:T(8,128)} copy(f32[3,2,256,8,64]{2,4,3,1,0:T(8,128)} %convolution_bitcast_fusion.13) | data formatting | bytes 6291456 | tf_op jit(solution)/shard_map/while/body/eval_jaxpr/ijhqk,ijqhd->ijkhd/transpose | solution.py:42
  227.0 6.2 %reshape.553 = f32[3,2,2,8,2,8,512]{6,5,4,3,2,1,0:T(8,128)} reshape(f32[3,2,256,8,64]{4,3,2,1,0:T(8,128)} %copy.203) | data formatting | bytes 6291456 | tf_op jit(solution)/shard_map/while/body/eval_jaxpr/reshape | solution.py:93
  244.9 8.3 %collective-permute-start.4 = (f32[2,2,32,4,512]{4,2,3,1,0:T(8,128)S(1)}, f32[2,2,32,4,512]{4,2,3,1,0:T(8,128)S(1)}, u32[]{:S(2)}, u32[]{:S(2)}) collective-permute-start(f32[2,2,32,4,512]{4,2,3,1,0:T(8,128)S(1)} %fusion.46), channel_id=1, source_target_pairs={{0,1},{1,2},{2,3},{3,4},{4,5},{5,6},{6,7},{8,9},{9,10},{10,11},{11... | collective-permute-start | bytes 3145736 | tf_op jit(solution)/shard_map/ppermute | solution.py:21
  257.2 13.4 %collective-permute-done.5 = f32[2,2,32,4,512]{4,2,3,1,0:T(8,128)S(1)} collective-permute-done((f32[2,2,32,4,512]{4,2,3,1,0:T(8,128)S(1)}, f32[2,2,32,4,512]{4,2,3,1,0:T(8,128)S(1)}, u32[]{:S(2)}, u32[]{:S(2)}) %collective-permute-start.5) | collective-permute-done | bytes 1048608 | tf_op jit(solution)/shard_map/ppermute | solution.py:21
  281.0 4.1 collective-permute-done.7
  285.6 3.2 convolution_bitcast_fusion.3
  293.0 157.2 %all-reduce.11.cloned.1.call-done = (f32[512,1536]{0,1:T(8,128)}, f32[512,512]{1,0:T(8,128)}) async-done(((f32[512,1536]{0,1:T(8,128)}, f32[512,512]{1,0:T(8,128)}), (f32[512,1536]{0,1:T(8,128)}, f32[512,512]{1,0:T(8,128)})) %all-reduce.11.cloned.1.call-update) | async-done | bytes 4194320 | tf_op jit(solution)/shard_map/psum | solution.py:248
  450.2 3.4 multiply_reduce_fusion.1
  (239 shorter events, 142.5 us)
Async XLA Ops:
  7.2 283.5 %copy-start = (bf16[512,1536]{1,0:T(8,128)(2,1)S(1)}, bf16[512,1536]{1,0:T(8,128)(2,1)}, u32[]{:S(2)}) copy-start(bf16[512,1536]{1,0:T(8,128)(2,1)} %param.20) | copy-start | bytes 4718596
  7.2 443.0 %all-reduce.11.cloned.1.call-start = ((), (), s32[]{:S(2)}) async-start(), calls=%async_computation | async-start | bytes 8388608 | tf_op jit(solution)/shard_map/psum | solution.py:248
  23.8 15.5 %collective-permute-start.1 = (bf16[2,2,4,16,512]{4,3,2,1,0:T(8,128)(2,1)}, bf16[2,2,4,16,512]{4,3,2,1,0:T(8,128)(2,1)S(1)}, u32[]{:S(2)}, u32[]{:S(2)}) collective-permute-start(bf16[2,2,4,16,512]{4,3,2,1,0:T(8,128)(2,1)} %get-tuple-element.294), channel_id=1, source_target_pairs={{8,0},{16,8},{24,16},{9,1},{17,9},{25,17},{10,2},{18,10},{26,18},{... | collective-permute-start | bytes 786440 | tf_op jit(solution)/shard_map/ppermute | solution.py:34
  25.1 14.2 %collective-permute-start = (bf16[2,2,4,16,512]{4,3,2,1,0:T(8,128)(2,1)}, bf16[2,2,4,16,512]{4,3,2,1,0:T(8,128)(2,1)}, u32[]{:S(2)}, u32[]{:S(2)}) collective-permute-start(bf16[2,2,4,16,512]{4,3,2,1,0:T(8,128)(2,1)} %get-tuple-element.293), channel_id=1, source_target_pairs={{0,8},{8,16},{16,24},{1,9},{9,17},{17,25},{2,10},{10,18},{18,26},{... | collective-permute-start | bytes 786440 | tf_op jit(solution)/shard_map/ppermute | solution.py:32
  33.6 3.8 copy-start.20
  37.4 7.9 %copy-start.23 = (bf16[512,512]{1,0:T(8,128)(2,1)S(1)}, bf16[512,512]{1,0:T(8,128)(2,1)}, u32[]{:S(2)}) copy-start(bf16[512,512]{1,0:T(8,128)(2,1)} %param.21) | copy-start | bytes 1572868
  37.8 9.1 %copy-start.14 = (f32[2,24,16,512]{3,2,1,0:T(8,128)S(1)}, f32[2,24,16,512]{3,2,1,0:T(8,128)}, u32[]{:S(2)}) copy-start(f32[2,24,16,512]{3,2,1,0:T(8,128)} %mul.131) | copy-start | bytes 4718596
  37.8 9.1 %copy-start.19 = (bf16[2,24,16,512]{3,2,1,0:T(8,128)(2,1)S(1)}, bf16[2,24,16,512]{3,2,1,0:T(8,128)(2,1)}, u32[]{:S(2)}) copy-start(bf16[2,24,16,512]{3,2,1,0:T(8,128)(2,1)} %param.22) | copy-start | bytes 2359300
  39.3 8.8 %copy-start.16 = (bf16[2,24,16,512]{3,2,1,0:T(8,128)(2,1)}, bf16[2,24,16,512]{3,2,1,0:T(8,128)(2,1)S(1)}, u32[]{:S(2)}) copy-start(bf16[2,24,16,512]{3,2,1,0:T(8,128)(2,1)S(1)} %broadcast_select_fusion) | copy-start | bytes 2359300
  41.0 7.1 %collective-permute-start.3 = (bf16[2,2,32,4,512]{4,3,2,1,0:T(4,128)(2,1)S(1)}, bf16[2,2,32,4,512]{4,3,2,1,0:T(4,128)(2,1)S(1)}, u32[]{:S(2)}, u32[]{:S(2)}) collective-permute-start(bf16[2,2,32,4,512]{4,3,2,1,0:T(4,128)(2,1)S(1)} %get-tuple-element.292), channel_id=1, source_target_pairs={{1,0},{2,1},{3,2},{4,3},{5,4},{6,5},{7,6},{9,8},{10,9},{11,10},{12... | collective-permute-start | bytes 1572872 | tf_op jit(solution)/shard_map/ppermute | solution.py:34
  42.3 5.8 %collective-permute-start.2 = (bf16[2,2,32,4,512]{4,3,2,1,0:T(4,128)(2,1)S(1)}, bf16[2,2,32,4,512]{4,3,2,1,0:T(4,128)(2,1)S(1)}, u32[]{:S(2)}, u32[]{:S(2)}) collective-permute-start(bf16[2,2,32,4,512]{4,3,2,1,0:T(4,128)(2,1)S(1)} %get-tuple-element.291), channel_id=1, source_target_pairs={{0,1},{1,2},{2,3},{3,4},{4,5},{5,6},{6,7},{8,9},{9,10},{10,11},{11... | collective-permute-start | bytes 1572872 | tf_op jit(solution)/shard_map/ppermute | solution.py:32
  63.5 4.5 copy-start.7
  81.8 4.4 copy-start.5
  81.8 4.4 copy-start.6
  99.8 3.1 copy-start.4
  140.7 2.8 copy-start.11
  158.6 4.5 copy-start.7
  176.9 4.4 copy-start.5
  176.9 4.4 copy-start.6
  195.0 3.1 copy-start.4
  235.9 2.8 copy-start.11
  243.4 9.8 %copy-start.10 = (f32[2,32,24,512]{3,1,2,0:T(8,128)S(1)}, f32[2,32,24,512]{3,1,2,0:T(8,128)}, u32[]{:S(2)}) copy-start(f32[2,32,24,512]{3,1,2,0:T(8,128)} %get-tuple-element.223) | copy-start | bytes 9437188
  243.5 9.8 %copy-start.13 = (f32[2,32,24,512]{3,1,2,0:T(8,128)S(1)}, f32[2,32,24,512]{3,1,2,0:T(8,128)}, u32[]{:S(2)}) copy-start(f32[2,32,24,512]{3,1,2,0:T(8,128)} %get-tuple-element.224) | copy-start | bytes 9437188
  244.9 10.5 %collective-permute-start.4 = (f32[2,2,32,4,512]{4,2,3,1,0:T(8,128)S(1)}, f32[2,2,32,4,512]{4,2,3,1,0:T(8,128)S(1)}, u32[]{:S(2)}, u32[]{:S(2)}) collective-permute-start(f32[2,2,32,4,512]{4,2,3,1,0:T(8,128)S(1)} %fusion.46), channel_id=1, source_target_pairs={{0,1},{1,2},{2,3},{3,4},{4,5},{5,6},{6,7},{8,9},{9,10},{10,11},{11... | collective-permute-start | bytes 3145736 | tf_op jit(solution)/shard_map/ppermute | solution.py:21
  255.8 19.5 %copy-start.17 = (bf16[2,24,16,512]{3,2,1,0:T(8,128)(2,1)S(1)}, bf16[2,24,16,512]{3,2,1,0:T(8,128)(2,1)}, u32[]{:S(2)}) copy-start(bf16[2,24,16,512]{3,2,1,0:T(8,128)(2,1)} %copy-done.16) | copy-start | bytes 2359300
  255.8 19.5 %copy-start.22 = (bf16[2,24,16,512]{3,2,1,0:T(8,128)(2,1)S(1)}, bf16[2,24,16,512]{3,2,1,0:T(8,128)(2,1)}, u32[]{:S(2)}) copy-start(bf16[2,24,16,512]{3,2,1,0:T(8,128)(2,1)} %get-tuple-element.225) | copy-start | bytes 2359300
  255.8 14.8 %collective-permute-start.5 = (f32[2,2,32,4,512]{4,2,3,1,0:T(8,128)S(1)}, f32[2,2,32,4,512]{4,2,3,1,0:T(8,128)S(1)}, u32[]{:S(2)}, u32[]{:S(2)}) collective-permute-start(f32[2,2,32,4,512]{4,2,3,1,0:T(8,128)S(1)} %get-tuple-element.283), channel_id=1, source_target_pairs={{1,0},{2,1},{3,2},{4,3},{5,4},{6,5},{7,6},{9,8},{10,9},{11,10},{12... | collective-permute-start | bytes 3145736 | tf_op jit(solution)/shard_map/ppermute | solution.py:21
  271.2 9.5 %collective-permute-start.6 = (f32[2,2,4,16,512]{4,2,3,1,0:T(4,128)S(1)}, f32[2,2,4,16,512]{4,2,3,1,0:T(4,128)S(1)}, u32[]{:S(2)}, u32[]{:S(2)}) collective-permute-start(f32[2,2,4,16,512]{4,2,3,1,0:T(4,128)S(1)} %get-tuple-element.286), channel_id=1, source_target_pairs={{0,8},{8,16},{16,24},{1,9},{9,17},{17,25},{2,10},{10,18},{18,26},{... | collective-permute-start | bytes 1572872 | tf_op jit(solution)/shard_map/ppermute | solution.py:21
  274.0 11.1 %collective-permute-start.7 = (f32[2,2,4,16,512]{4,2,3,1,0:T(4,128)S(1)}, f32[2,2,4,16,512]{4,2,3,1,0:T(4,128)S(1)}, u32[]{:S(2)}, u32[]{:S(2)}) collective-permute-start(f32[2,2,4,16,512]{4,2,3,1,0:T(4,128)S(1)} %get-tuple-element.285), channel_id=1, source_target_pairs={{8,0},{16,8},{24,16},{9,1},{17,9},{25,17},{10,2},{18,10},{26,18},{... | collective-permute-start | bytes 1572872 | tf_op jit(solution)/shard_map/ppermute | solution.py:21
  277.6 8.0 %copy-start.18 = (bf16[2,24,16,512]{3,1,2,0:T(8,128)(2,1)S(1)}, bf16[2,24,16,512]{3,1,2,0:T(8,128)(2,1)}, u32[]{:S(2)}) copy-start(bf16[2,24,16,512]{3,1,2,0:T(8,128)(2,1)} %get-tuple-element.222) | copy-start | bytes 2359300
  277.6 8.0 %copy-start.21 = (bf16[2,24,16,512]{3,2,1,0:T(8,128)(2,1)S(1)}, bf16[2,24,16,512]{3,2,1,0:T(8,128)(2,1)}, u32[]{:S(2)}) copy-start(bf16[2,24,16,512]{3,2,1,0:T(8,128)(2,1)} %param.19) | copy-start | bytes 2359300
  450.2 3.4 copy-start.15
  (16 other events, 31.0 us)
Sparse Core Ops, SparseCore 0:
  289.0 161.1 all-reduce.10
where the time goes:
time: 467 us; the launch traced here: 465 us
  waiting for transfers between devices  179 us (38%)
  local copies, waits for them, and re-layouts  162 us (35%)
  matrix products  43.7 us (9%)
  other arithmetic  37.7 us (8%)
  starting transfers between devices  25.9 us (6%)
  between operations  15.8 us (3%)
    psum x1, waiting for transfers between devices, body(): whole_qkv, whole_out = lax.psum((raw_qkv, raw_out), ('row', 'col'))  157 us
    dot_general x12, matrix products, product(): return jnp.einsum(form, left, right, preferred_element_type=jnp.float32)  35 us
    reshape x8, local copies, waits for them, and re-layouts, key_tiles(): paired.transpose(0, 2, 1, 3, 4)  27.9 us
    transpose x6, local copies, waits for them, and re-layouts, product(): return jnp.einsum(form, left, right, preferred_element_type=jnp.float32)  26.7 us
    reshape x4, local copies, waits for them, and re-layouts, fold_keys(): tile_set.reshape(tile_rows, tile_cols, 2, BLOCK, 2, BLOCK, features)  25 us
    ppermute x4, waiting for transfers between devices, passed_along(): return lax.ppermute(array, axis, pairs)  22 us
    while x54, local copies, waits for them, and re-layouts  18.2 us
    mul x9, local copies, waits for them, and re-layouts, dequantize(): mantissa.astype(jnp.float32)  17.7 us
  transfers between devices with their start and end apart: 9, of which 5 were waited for; matrix products, arithmetic and copies ran while one was open for 4% of the time, Pallas kernels for 0%

commit v1 on v0

v1 whole, which is shorter than its diff:
```python
import functools
import math

import jax
import jax.numpy as jnp
from jax import lax
from jax.experimental import pallas as pl
from jax.experimental.pallas import tpu as pltpu
from jax.sharding import PartitionSpec as P

HEADS = 8
RADIUS = 4
BLOCK = 8

max_norm = 1000.0
masked_score = -1e30
tiny_square = 1e-06
F32 = jnp.float32
BF16 = jnp.bfloat16


def dot(left, right, dims):
    return lax.dot_general(left, right, (dims, ((), ())), preferred_element_type=F32)


def prepare_kernel(q_ref, k_ref, v_ref, g_ref, fac_ref, crop_ref, w_ref,
                   q_out, kv_out, g_out, do_out, *, breadth):
    frame = pl.program_id(0)
    strip = pl.program_id(1)
    cells, features = q_ref.shape[1:]
    height = BLOCK * pl.num_programs(1)
    cell = lax.broadcasted_iota(jnp.int32, (cells, features), 0)
    block_col = (cell % breadth) // BLOCK

    def factor_of(which):
        factor = fac_ref[0, 0, 0:1, which * features:(which + 1) * features]
        full = jnp.broadcast_to(factor, (cells, features))
        for at in range(1, breadth // BLOCK):
            factor = fac_ref[0, 0, at:at + 1, which * features:(which + 1) * features]
            full = jnp.where(block_col == at, factor, full)
        return full

    q_out[0] = (q_ref[0].astype(F32) * factor_of(0)).astype(BF16)
    kv_out[0, 0] = (k_ref[0].astype(F32) * factor_of(1)).astype(BF16)
    kv_out[1, 0] = (v_ref[0].astype(F32) * factor_of(2)).astype(BF16)
    row = lax.axis_index("row") * height + strip * BLOCK + cell // breadth
    col = lax.axis_index("col") * breadth + cell % breadth
    inside = (row >= crop_ref[frame, 0]) & (col >= crop_ref[frame, 1])
    masked = jnp.where(inside, g_ref[0].astype(F32), 0.0).astype(BF16)
    g_out[0] = masked
    do_out[0] = dot(masked, w_ref[...], ((1,), (1,))).astype(BF16)


def prepare(q, k, v, g, factors, crop_start, w_out, breadth):
    members, cells, features = q.shape
    strip_cells = BLOCK * breadth
    strips = cells // strip_cells
    spec = pl.BlockSpec((1, strip_cells, features), lambda b, t: (b, t, 0))
    kv_spec = pl.BlockSpec((2, 1, strip_cells, features), lambda b, t: (0, b, t, 0))
    shape = jax.ShapeDtypeStruct(q.shape, BF16)
    return pl.pallas_call(
        functools.partial(prepare_kernel, breadth=breadth),
        grid=(members, strips),
        in_specs=[spec, spec, spec, spec,
                  pl.BlockSpec((1, 1) + factors.shape[2:], lambda b, t: (b, t, 0, 0)),
                  pl.BlockSpec(memory_space=pltpu.SMEM),
                  pl.BlockSpec(w_out.shape, lambda b, t: (0, 0))],
        out_specs=[spec, kv_spec, spec, spec],
        out_shape=[shape, jax.ShapeDtypeStruct((2,) + q.shape, BF16), shape, shape],
        name="prepare",
    )(q, k, v, g, factors, crop_start, w_out)


def attend_kernel(q_ref, do_ref, kvc_ref, kvs_ref, ot_ref, dq_ref, dc_ref, ds_ref, bias_ref,
                  *, breadth, head_dim):
    strip_cells = BLOCK * breadth
    side_cells = BLOCK * 2 * RADIUS
    strips = q_ref.shape[1] // strip_cells
    keys_c, keys_s = 2 * strip_cells, 2 * side_cells
    keys = keys_c + keys_s
    lanes = q_ref.shape[2]
    stacked = (lanes // head_dim) * strip_cells
    height = strips * BLOCK

    @pl.when((pl.program_id(0) == 0) & (pl.program_id(1) == 0))
    def _():
        key = lax.broadcasted_iota(jnp.int32, (keys, stacked), 0)
        query = lax.broadcasted_iota(jnp.int32, (keys, stacked), 1) % strip_cells
        side = key - keys_c
        key_row = jnp.where(key < keys_c, key // breadth, side // (2 * RADIUS)) - RADIUS
        along = side % (2 * RADIUS)
        key_col = jnp.where(
            key < keys_c, key % breadth,
            jnp.where(along < RADIUS, along - RADIUS, along - RADIUS + breadth))
        d_row = key_row - query // breadth
        d_col = key_col - query % breadth
        near = (jnp.abs(d_row) <= RADIUS) & (jnp.abs(d_col) <= RADIUS)
        frame_rows = height * lax.axis_size("row")
        frame_cols = breadth * lax.axis_size("col")
        at_col = key_col + lax.axis_index("col") * breadth
        near = near & (at_col >= 0) & (at_col < frame_cols)
        for strip in range(strips):
            at_row = key_row + strip * BLOCK + lax.axis_index("row") * height
            seen = near & (at_row >= 0) & (at_row < frame_rows)
            bias_ref[strip] = jnp.where(seen, 0.0, masked_score)

    lane = lax.broadcasted_iota(jnp.int32, (strip_cells, lanes), 1)
    masks = [jnp.where(lane // head_dim == h, 1.0, 0.0).astype(BF16)
             for h in range(lanes // head_dim)]
    scale = 1.0 / math.sqrt(head_dim)

    def by_head(whole):
        return jnp.concatenate(
            [whole[h * head_dim:(h + 1) * head_dim, h * strip_cells:(h + 1) * strip_cells]
             for h in range(lanes // head_dim)], 0)

    carry = None
    for strip in range(strips):
        at = slice(strip * strip_cells, (strip + 1) * strip_cells)
        at_c = slice(strip * strip_cells, strip * strip_cells + keys_c)
        at_s = slice(strip * side_cells, strip * side_cells + keys_s)
        q = q_ref[0, at] * scale
        g = do_ref[0, at]
        q_stack = jnp.concatenate([q * m for m in masks], 0)
        g_stack = jnp.concatenate([g * m for m in masks], 0)
        k = jnp.concatenate([kvc_ref[0, 0, at_c], kvs_ref[0, 0, at_s]], 0)
        v = jnp.concatenate([kvc_ref[1, 0, at_c], kvs_ref[1, 0, at_s]], 0)
        scores = dot(k, q_stack, ((1,), (1,))) + bias_ref[strip]
        weights = jnp.exp(scores - jnp.max(scores, axis=0, keepdims=True))
        softmax = weights * (1.0 / jnp.sum(weights, axis=0, keepdims=True))
        half = softmax.astype(BF16)
        grad_probs = dot(v, g_stack, ((1,), (1,)))
        delta = jnp.sum(softmax * grad_probs, axis=0, keepdims=True)
        grad_scores = (softmax * (grad_probs - delta)).astype(BF16)
        ot_ref[:, at] = by_head(dot(v, half, ((0,), (0,)))).astype(BF16)
        dq = by_head(dot(k, grad_scores, ((0,), (0,)))) * scale
        dq_ref[0, at] = dq.T.astype(BF16)
        parts = (dot(grad_scores, q_stack, ((1,), (0,))), dot(half, g_stack, ((1,), (0,))))
        for which in range(2):
            part_c, part_s = parts[which][:keys_c], parts[which][keys_c:]
            first_c, first_s = part_c[:strip_cells], part_s[:side_cells]
            if carry is not None:
                first_c = first_c + carry[which][0]
                first_s = first_s + carry[which][1]
            dc_ref[which, 0, at] = first_c
            ds_ref[which, 0, strip * side_cells:(strip + 1) * side_cells] = first_s.astype(BF16)
        carry = [(p[strip_cells:keys_c], p[keys_c + side_cells:]) for p in parts]
    for which in range(2):
        dc_ref[which, 0, strips * strip_cells:] = carry[which][0]
        ds_ref[which, 0, strips * side_cells:] = carry[which][1].astype(BF16)


def attend(q, do, kv_c, kv_s, breadth):
    members, cells, features = q.shape
    head_dim = features // HEADS
    lanes = 128
    strips = cells // (BLOCK * breadth)
    keys = 2 * BLOCK * (breadth + 2 * RADIUS)
    stacked = (lanes // head_dim) * BLOCK * breadth
    spec = pl.BlockSpec((1, cells, lanes), lambda b, h: (b, 0, h))

    def kv_spec(array):
        return pl.BlockSpec((2, 1, array.shape[2], lanes), lambda b, h: (0, b, 0, h))

    return pl.pallas_call(
        functools.partial(attend_kernel, breadth=breadth, head_dim=head_dim),
        grid=(members, features // lanes),
        in_specs=[spec, spec, kv_spec(kv_c), kv_spec(kv_s)],
        out_specs=[pl.BlockSpec((lanes, cells), lambda b, h: (h, b)), spec,
                   kv_spec(kv_c), kv_spec(kv_s)],
        out_shape=[jax.ShapeDtypeStruct((features, members * cells), BF16),
                   jax.ShapeDtypeStruct(q.shape, BF16),
                   jax.ShapeDtypeStruct(kv_c.shape, F32),
                   jax.ShapeDtypeStruct(kv_s.shape, BF16)],
        scratch_shapes=[pltpu.VMEM((strips, keys, stacked), F32)],
        name="attend",
    )(q, do, kv_c, kv_s)


def passed_along(array, axis, by):
    size = lax.axis_size(axis)
    return lax.ppermute(
        array, axis, [(i, i + by) for i in range(size) if 0 <= i + by < size])


def body(tokens, w_qkv, w_out, q_saved, k_saved, v_saved, scale_exp, grad_out, crop_start):
    members, height, breadth, features = tokens.shape
    cells = height * breadth
    rows, cols = lax.axis_size("row"), lax.axis_size("col")
    factors = jnp.repeat(jnp.exp2(scale_exp.astype(F32)), features // HEADS, axis=3)

    def flat(array):
        return array.reshape(members, cells, features)

    q, kv, g, do = prepare(flat(q_saved), flat(k_saved), flat(v_saved), flat(grad_out),
                           factors, crop_start, w_out, breadth)
    edge = RADIUS * breadth
    kv_c = jnp.concatenate(
        [passed_along(kv[:, :, -edge:], "row", 1), kv,
         passed_along(kv[:, :, :edge], "row", -1)], axis=2)
    grid = kv_c.reshape(2, members, height + 2 * RADIUS, breadth, features)
    kv_s = jnp.concatenate(
        [passed_along(grid[:, :, :, -RADIUS:], "col", 1),
         passed_along(grid[:, :, :, :RADIUS], "col", -1)], axis=3)
    kv_s = kv_s.reshape(2, members, -1, features)
    o_t, dq, d_c, d_s = attend(q, do, kv_c, kv_s, breadth)
    d_c = d_c.reshape(2, members, height + 2 * RADIUS, breadth, features)
    d_s = d_s.reshape(2, members, height + 2 * RADIUS, 2 * RADIUS, features)
    from_left = passed_along(d_s[:, :, :, RADIUS:], "col", 1)
    from_right = passed_along(d_s[:, :, :, :RADIUS], "col", -1)
    gap = jnp.zeros(d_s.shape[:3] + (breadth - 2 * RADIUS, features), BF16)
    d_c = d_c + jnp.concatenate([from_left, gap, from_right], axis=3).astype(F32)
    from_up = passed_along(d_c[:, :, -RADIUS:].astype(BF16), "row", 1)
    from_down = passed_along(d_c[:, :, :RADIUS].astype(BF16), "row", -1)
    gap = jnp.zeros((2, members, height - 2 * RADIUS, breadth, features), BF16)
    owned = d_c[:, :, RADIUS:-RADIUS] + jnp.concatenate(
        [from_up, gap, from_down], axis=2).astype(F32)
    owned = owned.astype(BF16).reshape(2, members * cells, features)
    flat_qkv = jnp.concatenate([dq.reshape(-1, features), owned[0], owned[1]], axis=1)
    grad_tokens = dot(flat_qkv, w_qkv, ((1,), (1,))).astype(BF16).reshape(tokens.shape)
    raw_qkv = dot(tokens.reshape(-1, features), flat_qkv, ((0,), (0,))).astype(BF16)
    raw_out = dot(o_t, g.reshape(-1, features), ((1,), (0,))).astype(BF16)
    pieces = jnp.concatenate(
        [raw.reshape(rows, features // rows, cols, -1).transpose(0, 2, 1, 3)
         for raw in (raw_qkv, raw_out)], axis=3)
    pieces = pieces.reshape((rows * cols,) + pieces.shape[2:])
    part = lax.psum_scatter(pieces, ("row", "col"), scatter_dimension=0, tiled=False)
    part = part.astype(F32)
    squares = lax.psum(jnp.sum(part * part), ("row", "col"))
    factor = jnp.minimum(1.0, max_norm / jnp.sqrt(squares + tiny_square))
    part = factor * part
    split = 3 * features // cols
    return grad_tokens, part[:, :split], part[:, split:]


def solution(mesh):
    placed = (
        P(None, "row", "col", None), P(), P(),
        P(None, "row", "col", None), P(None, "row", "col", None),
        P(None, "row", "col", None), P(None, "row", "col", None),
        P(None, "row", "col", None), P(),
    )
    return jax.shard_map(
        body, mesh=mesh, in_specs=placed,
        out_specs=(P(None, "row", "col", None), P("row", "col"), P("row", "col")),
        check_vma=False)
```

time: 467 us -> 305 us (0.65)
  local copies, waits for them, and re-layouts: 162 us -> 13.4 us
  matrix products: 43.7 us -> 6.64 us
  blocking collectives: 0 us -> 37 us
  Pallas kernels: 0 us -> 24.4 us
  other arithmetic: 37.7 us -> 14.3 us
  waiting for transfers between devices: 179 us -> 166 us
    psum x1 -> x0, waiting for transfers between devices: 157 us -> none  [body(): whole_qkv, whole_out = lax.psum((raw_qkv, raw_out), ('row', 'col'))]
    reduce_scatter x0 -> x1, waiting for transfers between devices: none -> 146 us  [body(): lax.psum_scatter(pieces, ('row', 'col'), scatter_dimension=0, tiled=False)]
    reshape x20 -> x3, local copies, waits for them, and re-layouts: 62.6 us -> 4.05 us  [the longest x2 3.3 us: body(): raw.reshape(rows, features // rows, cols, -1).transpose(0, 2, 1, 3)]
    dot_general x16 -> x3, matrix products: 43.7 us -> 6.64 us  [dot(): lax.dot_general(left, right, (dims, ((), ())), preferred_element_type=F32)]
    psum x0 -> x1, blocking collectives: none -> 37 us  [body(): squares = lax.psum(jnp.sum(part * part), ('row', 'col'))]
    transpose x14 -> x0, local copies, waits for them, and re-layouts: 27.4 us -> none  [the longest x6 26.7 us: product(): return jnp.einsum(form, left, right, preferred_element_type=jnp.float32)]
    pallas_call x0 -> x2, Pallas kernels: none -> 24.4 us  [the longest x1 17.8 us: attend(): pl.pallas_call(functools.partial(attend_kernel, breadth=breadth, head_dim...]
    while x54 -> x0, local copies, waits for them, and re-layouts: 18.2 us -> none
  transfers between devices with their start and end apart: 9 -> 9, of which waited for: 5 -> 8; matrix products, arithmetic and copies ran while one was open for 4% -> 1% of each run, Pallas kernels for 0% -> 0%
where the time goes in v1:
time: 305 us; the launch traced here: 304 us
  waiting for transfers between devices  166 us (54%)
  blocking collectives  37 us (12%)
  starting transfers between devices  27 us (9%)
  Pallas kernels  24.4 us (8%)
  between operations  15 us (5%)
  other arithmetic  14.3 us (5%)
  local copies, waits for them, and re-layouts  13.4 us (4%)
  matrix products  6.64 us (2%)
    reduce_scatter x1, waiting for transfers between devices, body(): lax.psum_scatter(pieces, ('row', 'col'), scatter_dimension=0, tiled=False)  146 us
    psum x1, blocking collectives, body(): squares = lax.psum(jnp.sum(part * part), ('row', 'col'))  37 us
    ppermute x8, starting transfers between devices, passed_along(): lax.ppermute(array, axis, [(i, i + by) for i in range(size) if 0 <= i + b...  26.9 us
    ppermute x8, waiting for transfers between devices, passed_along(): lax.ppermute(array, axis, [(i, i + by) for i in range(size) if 0 <= i + b...  20.1 us
    pallas_call x1, Pallas kernels, attend(): pl.pallas_call(functools.partial(attend_kernel, breadth=breadth, head_dim...  17.8 us
    dot_general x3, matrix products, dot(): lax.dot_general(left, right, (dims, ((), ())), preferred_element_type=F32)  6.64 us
    pallas_call x1, Pallas kernels, prepare(): pl.pallas_call(functools.partial(prepare_kernel, breadth=breadth), grid=(...  6.61 us
  transfers between devices with their start and end apart: 9, of which 8 were waited for; matrix products, arithmetic and copies ran while one was open for 1% of the time, Pallas kernels for 0%

profile of v1, /device:TPU:0, one launch (start us, length us, event | category | flops | bytes accessed | tf_op | source)
XLA Modules:
  0.0 303.8 jit_solution(13016580219876419625)
XLA Ops:
  7.2 0.8 multiply_exponential_fusion
  8.9 6.6 %prepare.1 = (bf16[2,384,512]{2,1,0:T(8,128)(2,1)}, bf16[2,2,384,512]{3,2,1,0:T(8,128)(2,1)}, bf16[2,384,512]{2,1,0:T(8,128)(2,1)}, bf16[2,384,512]{2,1,0:T(8,128)(2,1)}) custom-call(bf16[2,384,512]{2,1,0:T(8,128)(2,1)} %bitcast.38, bf16[2,384,512]{2,1,0:T(8,128)(2,1)} %bitcast.39, bf16[2,384,512]{2,1,0:T(8,128)(2,1)} %bitcast.40, ...), custom_call_target="tpu_custom_call" | custom-call | tf_op jit(solution)/shard_map/prepare/pallas_call | solution.py:61
  15.5 1.2 fusion.10
  16.7 5.0 %collective-permute-start = (bf16[2,2,64,512]{3,2,1,0:T(8,128)(2,1)S(1)}, bf16[2,2,64,512]{3,2,1,0:T(8,128)(2,1)S(1)}, u32[]{:S(2)}, u32[]{:S(2)}) collective-permute-start(bf16[2,2,64,512]{3,2,1,0:T(8,128)(2,1)S(1)} %get-tuple-element.28), channel_id=1, source_target_pairs={{0,8},{8,16},{16,24},{1,9},{9,17},{17,25},{2,10},{10,18},{18,26},{... | collective-permute-start | bytes 786440 | tf_op jit(solution)/shard_map/ppermute | solution.py:182
  21.7 1.3 collective-permute-start.1
  23.0 4.2 %collective-permute-done = bf16[2,2,64,512]{3,2,1,0:T(8,128)(2,1)S(1)} collective-permute-done((bf16[2,2,64,512]{3,2,1,0:T(8,128)(2,1)S(1)}, bf16[2,2,64,512]{3,2,1,0:T(8,128)(2,1)S(1)}, u32[]{:S(2)}, u32[]{:S(2)}) %collective-permute-start) | collective-permute-done | bytes 262176 | tf_op jit(solution)/shard_map/ppermute | solution.py:182
  27.4 4.0 %collective-permute-done.1 = bf16[2,2,64,512]{3,2,1,0:T(8,128)(2,1)S(1)} collective-permute-done((bf16[2,2,64,512]{3,2,1,0:T(8,128)(2,1)S(1)}, bf16[2,2,64,512]{3,2,1,0:T(8,128)(2,1)S(1)}, u32[]{:S(2)}, u32[]{:S(2)}) %collective-permute-start.1) | collective-permute-done | bytes 262176 | tf_op jit(solution)/shard_map/ppermute | solution.py:182
  31.8 1.3 collective-permute-start.2
  33.1 1.3 collective-permute-start.3
  34.6 4.0 %collective-permute-done.3 = bf16[2,2,32,4,512]{4,3,2,1,0:T(4,128)(2,1)S(1)} collective-permute-done((bf16[2,2,32,4,512]{4,3,2,1,0:T(4,128)(2,1)S(1)}, bf16[2,2,32,4,512]{4,3,2,1,0:T(4,128)(2,1)S(1)}, u32[]{:S(2)}, u32[]{:S(2)}) %collective-permute-start.3) | collective-permute-done | bytes 524320 | tf_op jit(solution)/shard_map/ppermute | solution.py:182
  38.6 1.5 maximum_bitcast_fusion.kvs_ref
  40.1 17.8 %attend.1 = (bf16[512,768]{1,0:T(8,128)(2,1)}, bf16[2,384,512]{2,1,0:T(8,128)(2,1)}, f32[2,2,512,512]{3,2,1,0:T(8,128)}, bf16[2,2,256,512]{3,2,1,0:T(8,128)(2,1)}) custom-call(bf16[2,384,512]{2,1,0:T(8,128)(2,1)} %get-tuple-element.11.q_ref, bf16[2,384,512]{2,1,0:T(8,128)(2,1)} %get-tuple-element.12.do_ref, bf16[2,2,512,512]{3,2,1,0:T(8,128)(2,1)} %copy-done.1, ...), custom_call_target="tpu_custom_call" | custom-call | tf_op jit(solution)/shard_map/attend/pallas_call | solution.py:165
  57.9 2.1 fusion.11
  60.0 12.0 %collective-permute-start.4 = (bf16[2,2,32,4,512]{4,3,2,1,0:T(4,128)(2,1)S(1)}, bf16[2,2,32,4,512]{4,3,2,1,0:T(4,128)(2,1)S(1)}, u32[]{:S(2)}, u32[]{:S(2)}) collective-permute-start(bf16[2,2,32,4,512]{4,3,2,1,0:T(4,128)(2,1)S(1)} %get-tuple-element.29), channel_id=1, source_target_pairs={{0,1},{1,2},{2,3},{3,4},{4,5},{5,6},{6,7},{8,9},{9,10},{10,11},{11... | collective-permute-start | bytes 1572872 | tf_op jit(solution)/shard_map/ppermute | solution.py:182
  72.0 1.3 collective-permute-start.5
  73.5 2.3 collective-permute-done.5
  75.8 5.6 %fusion.6 = (bf16[2,2,32,16,512]{4,3,2,1,0:T(8,128)(2,1)S(1)}, f32[2,2,32,16,512]{4,3,2,1,0:T(8,128)}) fusion(f32[2,2,32,16,512]{4,3,2,1,0:T(8,128)} %bitcast.35, bf16[2,2,32,4,512]{4,3,2,1,0:T(4,128)(2,1)S(1)} %collective-permute-done.5, bf16[16]{0:T(256)(128)(2,1)S(1)} %pad.9.clone, bf16[2,2,32,4,512]{4,3,2,1,0:T(4,128)(2,1)S(1)} %collective-permute-done.4), kind=kLoop, calls=%fused_computation.20 | loop fusion | flops 8388608 | bytes 11534368 | tf_op jit(solution)/shard_map/convert.1
  81.4 3.5 %collective-permute-start.6 = (bf16[2,2,4,16,512]{4,3,2,1,0:T(8,128)(2,1)S(1)}, bf16[2,2,4,16,512]{4,3,2,1,0:T(8,128)(2,1)S(1)}, u32[]{:S(2)}, u32[]{:S(2)}) collective-permute-start(bf16[2,2,4,16,512]{4,3,2,1,0:T(8,128)(2,1)S(1)} %get-tuple-element.21), channel_id=1, source_target_pairs={{0,8},{8,16},{16,24},{1,9},{9,17},{17,25},{2,10},{10,18},{18,26},{... | collective-permute-start | bytes 786440 | tf_op jit(solution)/shard_map/ppermute | solution.py:182
  84.9 1.3 collective-permute-start.7
  87.1 0.9 reshape.77
  88.0 0.8 collective-permute-done.6
  88.8 4.5 %collective-permute-done.7 = bf16[2,2,4,16,512]{4,3,2,1,0:T(8,128)(2,1)} collective-permute-done((bf16[2,2,4,16,512]{4,3,2,1,0:T(8,128)(2,1)S(1)}, bf16[2,2,4,16,512]{4,3,2,1,0:T(8,128)(2,1)}, u32[]{:S(2)}, u32[]{:S(2)}) %collective-permute-start.7) | collective-permute-done | bytes 262176 | tf_op jit(solution)/shard_map/ppermute | solution.py:182
  93.3 2.5 fusion
  96.0 0.9 copy-done.3
  97.7 2.6 fusion.1
  100.4 2.4 reshape.75
  102.7 2.4 pad_maximum_fusion.1
  105.1 1.8 copy.15
  107.0 146.0 %reduce-scatter.2.cloned.1.call-done = bf16[1,128,256]{1,2,0:T(8,128)(2,1)} async-done(((bf16[32,128,256]{1,2,0:T(8,128)(2,1)}), bf16[1,128,256]{1,2,0:T(8,128)(2,1)}) %reduce-scatter.2.cloned.1.call-update) | async-done | bytes 65552 | tf_op jit(solution)/shard_map/reduce_scatter | solution.py:227
  253.0 1.5 fusion.2
  254.5 3.5 %convolution_convert_fusion.1 = bf16[768,512]{1,0:T(8,128)(2,1)} fusion(bf16[512,1536]{1,0:T(8,128)(2,1)S(1)} %copy-done, bf16[768,512]{1,0:T(8,128)(2,1)S(1)} %bitcast.45, bf16[768,512]{1,0:T(8,128)(2,1)S(1)} %bitcast.43, bf16[768,512]{1,0:T(8,128)(2,1)} %bitcast.48), kind=kOutput, calls=%fused_computation.7 | convolution fusion | flops 1215430656 | bytes 4718592 | tf_op jit(solution)/shard_map/dot_general | solution.py:23
  258.0 37.0 %psum.7 = f32[]{:T(128)} all-reduce(f32[]{:T(128)} %fusion.2), channel_id=1, replica_groups=mesh['row'=4,'col'=8] {'row','col'}, use_global_device_ids=true, to_apply=%region_2.0 | all-reduce | flops 1 | bytes 8 | tf_op jit(solution)/shard_map/psum | solution.py:229
  (44 shorter events, 5.0 us)
Async XLA Ops:
  7.2 247.3 %copy-start = (bf16[512,1536]{1,0:T(8,128)(2,1)S(1)}, bf16[512,1536]{1,0:T(8,128)(2,1)}, u32[]{:S(2)}) copy-start(bf16[512,1536]{1,0:T(8,128)(2,1)} %param.10) | copy-start | bytes 4718596
  7.2 245.8 %reduce-scatter.2.cloned.1.call-start = ((), (), s32[]{:S(2)}) async-start(), calls=%async_computation.1 | async-start | bytes 2162688 | tf_op jit(solution)/shard_map/reduce_scatter | solution.py:227
  15.5 11.7 %copy-start.2 = (bf16[2,2,384,512]{3,2,1,0:T(8,128)(2,1)S(1)}, bf16[2,2,384,512]{3,2,1,0:T(8,128)(2,1)}, u32[]{:S(2)}) copy-start(bf16[2,2,384,512]{3,2,1,0:T(8,128)(2,1)} %get-tuple-element.13) | copy-start | bytes 4718596
  16.7 10.5 %collective-permute-start = (bf16[2,2,64,512]{3,2,1,0:T(8,128)(2,1)S(1)}, bf16[2,2,64,512]{3,2,1,0:T(8,128)(2,1)S(1)}, u32[]{:S(2)}, u32[]{:S(2)}) collective-permute-start(bf16[2,2,64,512]{3,2,1,0:T(8,128)(2,1)S(1)} %get-tuple-element.28), channel_id=1, source_target_pairs={{0,8},{8,16},{16,24},{1,9},{9,17},{17,25},{2,10},{10,18},{18,26},{... | collective-permute-start | bytes 786440 | tf_op jit(solution)/shard_map/ppermute | solution.py:182
  21.7 9.7 %collective-permute-start.1 = (bf16[2,2,64,512]{3,2,1,0:T(8,128)(2,1)S(1)}, bf16[2,2,64,512]{3,2,1,0:T(8,128)(2,1)S(1)}, u32[]{:S(2)}, u32[]{:S(2)}) collective-permute-start(bf16[2,2,64,512]{3,2,1,0:T(8,128)(2,1)S(1)} %get-tuple-element.27), channel_id=1, source_target_pairs={{8,0},{16,8},{24,16},{9,1},{17,9},{25,17},{10,2},{18,10},{26,18},{... | collective-permute-start | bytes 786440 | tf_op jit(solution)/shard_map/ppermute | solution.py:182
  31.4 8.7 %copy-start.1 = (bf16[2,2,512,512]{3,2,1,0:T(8,128)(2,1)}, bf16[2,2,512,512]{3,2,1,0:T(8,128)(2,1)S(1)}, u32[]{:S(2)}) copy-start(bf16[2,2,512,512]{3,2,1,0:T(8,128)(2,1)S(1)} %constant_dynamic-update-slice_fusion.kvc_ref) | copy-start | bytes 6291460
  31.8 2.8 collective-permute-start.2
  33.1 5.5 %collective-permute-start.3 = (bf16[2,2,32,4,512]{4,3,2,1,0:T(4,128)(2,1)S(1)}, bf16[2,2,32,4,512]{4,3,2,1,0:T(4,128)(2,1)S(1)}, u32[]{:S(2)}, u32[]{:S(2)}) collective-permute-start(bf16[2,2,32,4,512]{4,3,2,1,0:T(4,128)(2,1)S(1)} %get-tuple-element.24), channel_id=1, source_target_pairs={{1,0},{2,1},{3,2},{4,3},{5,4},{6,5},{7,6},{9,8},{10,9},{11,10},{12... | collective-permute-start | bytes 1572872 | tf_op jit(solution)/shard_map/ppermute | solution.py:182
  60.0 13.5 %collective-permute-start.4 = (bf16[2,2,32,4,512]{4,3,2,1,0:T(4,128)(2,1)S(1)}, bf16[2,2,32,4,512]{4,3,2,1,0:T(4,128)(2,1)S(1)}, u32[]{:S(2)}, u32[]{:S(2)}) collective-permute-start(bf16[2,2,32,4,512]{4,3,2,1,0:T(4,128)(2,1)S(1)} %get-tuple-element.29), channel_id=1, source_target_pairs={{0,1},{1,2},{2,3},{3,4},{4,5},{5,6},{6,7},{8,9},{9,10},{10,11},{11... | collective-permute-start | bytes 1572872 | tf_op jit(solution)/shard_map/ppermute | solution.py:182
  72.0 3.8 %collective-permute-start.5 = (bf16[2,2,32,4,512]{4,3,2,1,0:T(4,128)(2,1)S(1)}, bf16[2,2,32,4,512]{4,3,2,1,0:T(4,128)(2,1)S(1)}, u32[]{:S(2)}, u32[]{:S(2)}) collective-permute-start(bf16[2,2,32,4,512]{4,3,2,1,0:T(4,128)(2,1)S(1)} %get-tuple-element.30), channel_id=1, source_target_pairs={{1,0},{2,1},{3,2},{4,3},{5,4},{6,5},{7,6},{9,8},{10,9},{11,10},{12... | collective-permute-start | bytes 1572872 | tf_op jit(solution)/shard_map/ppermute | solution.py:182
  75.8 10.5 %copy-start.9 = (bf16[2,384,512]{2,1,0:T(8,128)(2,1)S(1)}, bf16[2,384,512]{2,1,0:T(8,128)(2,1)}, u32[]{:S(2)}) copy-start(bf16[2,384,512]{2,1,0:T(8,128)(2,1)} %get-tuple-element.18) | copy-start | bytes 2359300
  75.8 10.5 %copy-start.11 = (bf16[512,768]{1,0:T(8,128)(2,1)S(1)}, bf16[512,768]{1,0:T(8,128)(2,1)}, u32[]{:S(2)}) copy-start(bf16[512,768]{1,0:T(8,128)(2,1)} %get-tuple-element.17) | copy-start | bytes 2359300
  81.4 7.4 %collective-permute-start.6 = (bf16[2,2,4,16,512]{4,3,2,1,0:T(8,128)(2,1)S(1)}, bf16[2,2,4,16,512]{4,3,2,1,0:T(8,128)(2,1)S(1)}, u32[]{:S(2)}, u32[]{:S(2)}) collective-permute-start(bf16[2,2,4,16,512]{4,3,2,1,0:T(8,128)(2,1)S(1)} %get-tuple-element.21), channel_id=1, source_target_pairs={{0,8},{8,16},{16,24},{1,9},{9,17},{17,25},{2,10},{10,18},{18,26},{... | collective-permute-start | bytes 786440 | tf_op jit(solution)/shard_map/ppermute | solution.py:182
  84.9 8.4 %collective-permute-start.7 = (bf16[2,2,4,16,512]{4,3,2,1,0:T(8,128)(2,1)S(1)}, bf16[2,2,4,16,512]{4,3,2,1,0:T(8,128)(2,1)}, u32[]{:S(2)}, u32[]{:S(2)}) collective-permute-start(bf16[2,2,4,16,512]{4,3,2,1,0:T(8,128)(2,1)S(1)} %get-tuple-element.22), channel_id=1, source_target_pairs={{8,0},{16,8},{24,16},{9,1},{17,9},{25,17},{10,2},{18,10},{26,18},{... | collective-permute-start | bytes 786440 | tf_op jit(solution)/shard_map/ppermute | solution.py:182
  95.8 1.3 copy-start.8
  95.8 1.9 copy-start.10
  96.0 0.9 copy-start.3
  96.0 1.1 copy-start.5
  106.9 147.5 %copy-start.4 = (bf16[1,2,24,16,512]{4,3,2,1,0:T(8,128)(2,1)S(1)}, bf16[1,2,24,16,512]{4,3,2,1,0:T(8,128)(2,1)}, u32[]{:S(2)}) copy-start(bf16[1,2,24,16,512]{4,3,2,1,0:T(8,128)(2,1)} %copy-done.3) | copy-start | bytes 2359300
  107.0 147.5 %copy-start.6 = (bf16[1,2,24,16,512]{4,3,2,1,0:T(8,128)(2,1)S(1)}, bf16[1,2,24,16,512]{4,3,2,1,0:T(8,128)(2,1)}, u32[]{:S(2)}) copy-start(bf16[1,2,24,16,512]{4,3,2,1,0:T(8,128)(2,1)} %copy-done.5) | copy-start | bytes 2359300
  254.5 41.2 %copy-start.7 = (bf16[1,128,256]{1,2,0:T(8,128)(2,1)S(1)}, bf16[1,128,256]{1,2,0:T(8,128)(2,1)}, u32[]{:S(2)}) copy-start(bf16[1,128,256]{1,2,0:T(8,128)(2,1)} %reduce-scatter.2.cloned.1.call-done) | copy-start | bytes 196612
Sparse Core Ops, SparseCore 0:
  107.1 145.8 reduce-scatter.1

commit v2 on v1

--- a/solution.py
+++ b/solution.py
@@ -177,6 +177,183 @@
     )(q, do, kv_c, kv_s)
 
 
+def bits_of(count):
+    return max(count.bit_length() - 1, 0)
+
+
+def halving_orders(rows, cols):
+    col = [("col", k) for k in range(bits_of(cols))]
+    row = [("row", k) for k in range(bits_of(rows))]
+    return [col[:1] + col[1:] + row, col[:1] + col[:0:-1] + row]
+
+
+def col_place(order, col):
+    place = 0
+    for axis, bit in order:
+        if axis == "col":
+            place = 2 * place + (col >> bit) % 2
+    return place
+
+
+def weights_kernel(tok_ref, ot_ref, dq_ref, dk_ref, dv_ref, g_ref, w_ref,
+                   dq_rows, dk_rows, dv_rows, gt_ref, buf_ref, *, orders, rows, cols):
+    features = g_ref.shape[1]
+    tok = tok_ref[...]
+    raw = jnp.concatenate(
+        [dot(tok, ref[...], ((0,), (0,))) for ref in (dq_ref, dk_ref, dv_ref)], 1)
+    raw_out = dot(ot_ref[...], g_ref[...], ((1,), (0,)))
+    wide, narrow = 3 * features // cols, features // cols
+    part_rows = buf_ref.shape[3]
+    group = tok.shape[1] // (2 * part_rows)
+    nbits = bits_of(rows)
+    for member, col in ((m, c) for m in range(group) for c in range(cols)):
+        row = pl.program_id(0) * group + member
+        place = sum(((row // 2 ** k) % 2) * 2 ** (nbits - 1 - k) for k in range(nbits))
+        piece = jnp.concatenate(
+            [raw[:, col * wide:(col + 1) * wide], raw_out[:, col * narrow:(col + 1) * narrow]],
+            1).astype(BF16)
+        for half, order in enumerate(orders):
+            first = (2 * member + half) * part_rows
+            buf_ref[half, col_place(order, col), place] = piece[first:first + part_rows]
+    total = dot(dq_rows[...], w_ref[:, :features], ((1,), (1,)))
+    total = total + dot(dk_rows[...], w_ref[:, features:2 * features], ((1,), (1,)))
+    total = total + dot(dv_rows[...], w_ref[:, 2 * features:], ((1,), (1,)))
+    gt_ref[...] = total.astype(BF16)
+
+
+def weight_pieces(tokens, o_t, dq, dk, dv, g, w_qkv, rows, cols):
+    cells, features = tokens.shape
+    orders = halving_orders(rows, cols)
+    part_rows = features // rows
+    group = max(1, 128 // part_rows)
+    whole = pl.BlockSpec((cells, features), lambda r: (0, 0))
+    some = pl.BlockSpec((cells * group // rows, features), lambda r: (r, 0))
+    lanes = 4 * features // cols
+    return pl.pallas_call(
+        functools.partial(weights_kernel, orders=orders, rows=rows, cols=cols),
+        grid=(rows // group,),
+        in_specs=[pl.BlockSpec((cells, group * part_rows), lambda r: (0, r)),
+                  pl.BlockSpec((group * part_rows, cells), lambda r: (r, 0)),
+                  whole, whole, whole, whole,
+                  pl.BlockSpec(w_qkv.shape, lambda r: (0, 0)), some, some, some],
+        out_specs=[some, pl.BlockSpec((2, cols, rows, part_rows // 2, lanes),
+                                      lambda r: (0, 0, 0, 0, 0))],
+        out_shape=[jax.ShapeDtypeStruct((cells, features), BF16),
+                   jax.ShapeDtypeStruct((2, cols, rows, part_rows // 2, lanes), BF16)],
+        name="weights",
+    )(tokens, o_t, dq, dk, dv, g, w_qkv, dq, dk, dv)
+
+
+def reduce_kernel(buf_ref, qkv_ref, out_ref, work, recv, own_sq, all_sq,
+                  send_sem, recv_sem, sq_send, sq_recv, *, rows, cols):
+    orders = halving_orders(rows, cols)
+    count = rows * cols
+    mine = {"row": lax.axis_index("row"), "col": lax.axis_index("col")}
+    me = mine["row"] * cols + mine["col"]
+
+    def other(i):
+        at = lax.rem(me + i, count)
+        return (at // cols, at % cols)
+
+    barrier = pltpu.get_barrier_semaphore()
+
+    def greet(i, _):
+        pl.semaphore_signal(barrier, inc=1, device_id=other(i),
+                            device_id_type=pl.DeviceIdType.MESH)
+        return 0
+
+    lax.fori_loop(1, count, greet, 0)
+    pl.semaphore_wait(barrier, count - 1)
+    steps = len(orders[0])
+    base = [0, 0]
+    finals = [None, None]
+
+    def start(half, step):
+        axis, bit = orders[half][step]
+        size = count >> (step + 1)
+        mybit = (mine[axis] // 2 ** bit) % 2
+        partner = dict(mine)
+        partner[axis] = mine[axis] + (1 - 2 * mybit) * 2 ** bit
+        source = buf_ref if step == 0 else work
+        at = recv.at[half, pl.ds(count - 2 * size, size)]
+        copy = pltpu.make_async_remote_copy(
+            src_ref=source.at[half, pl.ds(base[half] + (1 - mybit) * size, size)],
+            dst_ref=at, send_sem=send_sem.at[half, step], recv_sem=recv_sem.at[half, step],
+            device_id=(partner["row"], partner["col"]),
+            device_id_type=pl.DeviceIdType.MESH)
+        copy.start()
+        return copy, size, mybit
+
+    flights = [start(half, 0) for half in range(2)]
+    for step in range(steps):
+        for half in range(2):
+            copy, size, mybit = flights[half]
+            copy.wait()
+            keep = base[half] + mybit * size
+            first = count - 2 * size
+            if step == steps - 1:
+                finals[half] = work[half, keep].astype(F32) + recv[half, first].astype(F32)
+                continue
+            source = buf_ref if step == 0 else work
+            base[half] = 0 if step == 0 else keep
+
+            def add(i, _, half=half, keep=keep, first=first, source=source, to=base[half]):
+                work[half, to + i] = (source[half, keep + i].astype(F32)
+                                      + recv[half, first + i].astype(F32)).astype(BF16)
+                return 0
+
+            lax.fori_loop(0, size, add, 0)
+            flights[half] = start(half, step + 1)
+    part = jnp.concatenate(finals, 0)
+    squares = jnp.sum((part * part).reshape(-1, 8, part.shape[1]), axis=0)
+    tile = own_sq.shape[1]
+    own_sq[...] = sum(squares[:, j * tile:(j + 1) * tile] for j in range(part.shape[1] // tile))
+
+    def square_copy(i):
+        return pltpu.make_async_remote_copy(
+            src_ref=own_sq, dst_ref=all_sq.at[i], send_sem=sq_send.at[i],
+            recv_sem=sq_recv.at[i], device_id=other(i),
+            device_id_type=pl.DeviceIdType.MESH)
+
+    def send(i, _):
+        square_copy(i).start()
+        return 0
+
+    def take(i, total):
+        square_copy(i).wait()
+        return total + all_sq[i]
+
+    lax.fori_loop(1, count, send, 0)
+    total = jnp.sum(lax.fori_loop(1, count, take, own_sq[...]), keepdims=True)
+    factor = jnp.minimum(1.0, max_norm / jnp.sqrt(total + tiny_square))
+    part = part * factor
+    split = qkv_ref.shape[1]
+    qkv_ref[...] = part[:, :split]
+    out_ref[...] = part[:, split:]
+
+
+def reduce_pieces(pieces, rows, cols):
+    count = rows * cols
+    half_rows, lanes = pieces.shape[3:]
+    pieces = pieces.reshape(2, count, half_rows, lanes)
+    steps = bits_of(count)
+    vmem = pl.BlockSpec(memory_space=pltpu.VMEM)
+    return pl.pallas_call(
+        functools.partial(reduce_kernel, rows=rows, cols=cols),
+        in_specs=[vmem], out_specs=[vmem, vmem],
+        out_shape=[jax.ShapeDtypeStruct((2 * half_rows, 3 * lanes // 4), F32),
+                   jax.ShapeDtypeStruct((2 * half_rows, lanes // 4), F32)],
+        scratch_shapes=[
+            pltpu.VMEM((2, count // 2, half_rows, lanes), BF16),
+            pltpu.VMEM((2, count, half_rows, lanes), BF16),
+            pltpu.VMEM((8, 128), F32), pltpu.VMEM((count, 8, 128), F32),
+            pltpu.SemaphoreType.DMA((2, steps)), pltpu.SemaphoreType.DMA((2, steps)),
+            pltpu.SemaphoreType.DMA((count,)), pltpu.SemaphoreType.DMA((count,))],
+        compiler_params=pltpu.CompilerParams(collective_id=1, has_side_effects=True),
+        name="reduce",
+    )(pieces)
+
+
 def passed_along(array, axis, by):
     size = lax.axis_size(axis)
     return lax.ppermute(
@@ -216,21 +393,11 @@
     owned = d_c[:, :, RADIUS:-RADIUS] + jnp.concatenate(
         [from_up, gap, from_down], axis=2).astype(F32)
     owned = owned.astype(BF16).reshape(2, members * cells, features)
-    flat_qkv = jnp.concatenate([dq.reshape(-1, features), owned[0], owned[1]], axis=1)
-    grad_tokens = dot(flat_qkv, w_qkv, ((1,), (1,))).astype(BF16).reshape(tokens.shape)
-    raw_qkv = dot(tokens.reshape(-1, features), flat_qkv, ((0,), (0,))).astype(BF16)
-    raw_out = dot(o_t, g.reshape(-1, features), ((1,), (0,))).astype(BF16)
-    pieces = jnp.concatenate(
-        [raw.reshape(rows, features // rows, cols, -1).transpose(0, 2, 1, 3)
-         for raw in (raw_qkv, raw_out)], axis=3)
-    pieces = pieces.reshape((rows * cols,) + pieces.shape[2:])
-    part = lax.psum_scatter(pieces, ("row", "col"), scatter_dimension=0, tiled=False)
-    part = part.astype(F32)
-    squares = lax.psum(jnp.sum(part * part), ("row", "col"))
-    factor = jnp.minimum(1.0, max_norm / jnp.sqrt(squares + tiny_square))
-    part = factor * part
-    split = 3 * features // cols
-    return grad_tokens, part[:, :split], part[:, split:]
+    grad_tokens, pieces = weight_pieces(
+        tokens.reshape(-1, features), o_t, dq.reshape(-1, features), owned[0], owned[1],
+        g.reshape(-1, features), w_qkv, rows, cols)
+    grad_qkv, grad_out_w = reduce_pieces(pieces, rows, cols)
+    return grad_tokens.reshape(tokens.shape), grad_qkv, grad_out_w
 
 
 def solution(mesh):

time: 305 us -> 143 us (0.47)
  waiting for transfers between devices: 166 us -> 14.9 us
  Pallas kernels: 24.4 us -> 83.5 us
  blocking collectives: 37 us -> 0 us
  between operations: 15 us -> 0.82 us
  other arithmetic: 14.3 us -> 6.06 us
  matrix products: 6.64 us -> 0 us
  local copies, waits for them, and re-layouts: 13.4 us -> 9.29 us
    reduce_scatter x1 -> x0, waiting for transfers between devices: 146 us -> none  [body(): lax.psum_scatter(pieces, ('row', 'col'), scatter_dimension=0, tiled=False)]
    pallas_call x0 -> x2, Pallas kernels: none -> 59.1 us  [the longest x1 50.3 us: reduce_pieces(): pl.pallas_call(functools.partial(reduce_kernel, rows=rows, cols=cols), in...]
    psum x1 -> x0, blocking collectives: 37 us -> none  [body(): squares = lax.psum(jnp.sum(part * part), ('row', 'col'))]
    dot_general x3 -> x0, matrix products: 6.64 us -> none  [dot(): lax.dot_general(left, right, (dims, ((), ())), preferred_element_type=F32)]
    ppermute x8, waiting for transfers between devices: 20.1 us -> 14.9 us  [passed_along(): lax.ppermute(array, axis, [(i, i + by) for i in range(size) if 0 <= i + b...]
    reshape x2 -> x0, local copies, waits for them, and re-layouts: 3.3 us -> none  [body(): raw.reshape(rows, features // rows, cols, -1).transpose(0, 2, 1, 3)]
  transfers between devices with their start and end apart: 9 -> 8, of which waited for: 8 -> 6; matrix products, arithmetic and copies ran while one was open for 1% -> 0% of each run, Pallas kernels for 0% -> 0%
where the time goes in v2:
time: 143 us; the launch traced here: 142 us
  Pallas kernels  83.5 us (58%)
  starting transfers between devices  27.6 us (19%)
  waiting for transfers between devices  14.9 us (10%)
  local copies, waits for them, and re-layouts  9.29 us (6%)
  other arithmetic  6.06 us (4%)
    pallas_call x1, Pallas kernels, reduce_pieces(): pl.pallas_call(functools.partial(reduce_kernel, rows=rows, cols=cols), in...  50.3 us
    ppermute x8, starting transfers between devices, passed_along(): lax.ppermute(array, axis, [(i, i + by) for i in range(size) if 0 <= i + b...  27.6 us
    pallas_call x1, Pallas kernels, attend(): pl.pallas_call(functools.partial(attend_kernel, breadth=breadth, head_dim...  17.8 us
    ppermute x8, waiting for transfers between devices, passed_along(): lax.ppermute(array, axis, [(i, i + by) for i in range(size) if 0 <= i + b...  14.9 us
    pallas_call x1, Pallas kernels, weight_pieces(): pl.pallas_call(functools.partial(weights_kernel, orders=orders, rows=rows...  8.75 us
    pallas_call x1, Pallas kernels, prepare(): pl.pallas_call(functools.partial(prepare_kernel, breadth=breadth), grid=(...  6.59 us
    unnamed x8, local copies, waits for them, and re-layouts  3.31 us
    another operation x1, other arithmetic  3.26 us
  transfers between devices with their start and end apart: 8, of which 6 were waited for; matrix products, arithmetic and copies ran while one was open for 0% of the time, Pallas kernels for 0%

profile of v2, /device:TPU:0, one launch (start us, length us, event | category | flops | bytes accessed | tf_op | source)
XLA Modules:
  0.0 142.1 jit_solution(4799172245025099923)
XLA Ops:
  0.6 0.7 multiply_exponential_fusion
  1.3 0.1 broadcast_in_dim.9
  1.4 0.8 reshape.58.fac_ref
  2.2 6.6 %prepare.1 = (bf16[2,384,512]{2,1,0:T(8,128)(2,1)}, bf16[2,2,384,512]{3,2,1,0:T(8,128)(2,1)}, bf16[2,384,512]{2,1,0:T(8,128)(2,1)}, bf16[2,384,512]{2,1,0:T(8,128)(2,1)}) custom-call(bf16[2,384,512]{2,1,0:T(8,128)(2,1)} %bitcast.30, bf16[2,384,512]{2,1,0:T(8,128)(2,1)} %bitcast.31, bf16[2,384,512]{2,1,0:T(8,128)(2,1)} %bitcast.32, ...), custom_call_target="tpu_custom_call" | custom-call | tf_op jit(solution)/shard_map/prepare/pallas_call | solution.py:61
  8.8 1.2 fusion.5
  10.0 5.0 %collective-permute-start = (bf16[2,2,64,512]{3,2,1,0:T(8,128)(2,1)S(1)}, bf16[2,2,64,512]{3,2,1,0:T(8,128)(2,1)S(1)}, u32[]{:S(2)}, u32[]{:S(2)}) collective-permute-start(bf16[2,2,64,512]{3,2,1,0:T(8,128)(2,1)S(1)} %get-tuple-element.39), channel_id=1, source_target_pairs={{0,8},{8,16},{16,24},{1,9},{9,17},{17,25},{2,10},{10,18},{18,26},{... | collective-permute-start | bytes 786440 | tf_op jit(solution)/shard_map/ppermute | solution.py:359
  15.0 1.3 collective-permute-start.1
  16.3 4.2 %collective-permute-done = bf16[2,2,64,512]{3,2,1,0:T(8,128)(2,1)S(1)} collective-permute-done((bf16[2,2,64,512]{3,2,1,0:T(8,128)(2,1)S(1)}, bf16[2,2,64,512]{3,2,1,0:T(8,128)(2,1)S(1)}, u32[]{:S(2)}, u32[]{:S(2)}) %collective-permute-start) | collective-permute-done | bytes 262176 | tf_op jit(solution)/shard_map/ppermute | solution.py:359
  20.5 0.1 constant_dynamic-update-slice_fusion.1
  20.6 4.0 %collective-permute-done.1 = bf16[2,2,64,512]{3,2,1,0:T(8,128)(2,1)S(1)} collective-permute-done((bf16[2,2,64,512]{3,2,1,0:T(8,128)(2,1)S(1)}, bf16[2,2,64,512]{3,2,1,0:T(8,128)(2,1)S(1)}, u32[]{:S(2)}, u32[]{:S(2)}) %collective-permute-start.1) | collective-permute-done | bytes 262176 | tf_op jit(solution)/shard_map/ppermute | solution.py:359
  24.6 0.4 fusion.3
  25.1 1.3 collective-permute-start.3
  26.4 3.1 %collective-permute-start.2 = (bf16[2,2,32,4,512]{4,3,2,1,0:T(4,128)(2,1)S(1)}, bf16[2,2,32,4,512]{4,3,2,1,0:T(4,128)(2,1)S(1)}, u32[]{:S(2)}, u32[]{:S(2)}) collective-permute-start(bf16[2,2,32,4,512]{4,3,2,1,0:T(4,128)(2,1)S(1)} %get-tuple-element.34), channel_id=1, source_target_pairs={{0,1},{1,2},{2,3},{3,4},{4,5},{5,6},{6,7},{8,9},{9,10},{10,11},{11... | collective-permute-start | bytes 1572872 | tf_op jit(solution)/shard_map/ppermute | solution.py:359
  29.4 1.5 %collective-permute-done.2 = bf16[2,2,32,4,512]{4,3,2,1,0:T(4,128)(2,1)S(1)} collective-permute-done((bf16[2,2,32,4,512]{4,3,2,1,0:T(4,128)(2,1)S(1)}, bf16[2,2,32,4,512]{4,3,2,1,0:T(4,128)(2,1)S(1)}, u32[]{:S(2)}, u32[]{:S(2)}) %collective-permute-start.2) | collective-permute-done | bytes 524320 | tf_op jit(solution)/shard_map/ppermute | solution.py:359
  30.9 1.5 %maximum_bitcast_fusion.kvs_ref = bf16[2,2,256,512]{3,2,1,0:T(8,128)(2,1)} fusion(bf16[2,2,32,4,512]{4,3,2,1,0:T(4,128)(2,1)S(1)} %collective-permute-done.3, bf16[2,2,32,4,512]{4,3,2,1,0:T(4,128)(2,1)S(1)} %collective-permute-done.2), kind=kLoop, calls=%fused_computation.3 | loop fusion | flops 2097152 | bytes 2097152 | tf_op jit(solution)/shard_map/reshape | solution.py:382
  32.4 17.8 %attend.1 = (bf16[512,768]{1,0:T(8,128)(2,1)}, bf16[2,384,512]{2,1,0:T(8,128)(2,1)}, f32[2,2,512,512]{3,2,1,0:T(8,128)}, bf16[2,2,256,512]{3,2,1,0:T(8,128)(2,1)}) custom-call(bf16[2,384,512]{2,1,0:T(8,128)(2,1)} %get-tuple-element.15.q_ref, bf16[2,384,512]{2,1,0:T(8,128)(2,1)} %get-tuple-element.16.do_ref, bf16[2,2,512,512]{3,2,1,0:T(8,128)(2,1)} %copy-done, ...), custom_call_target="tpu_custom_call" | custom-call | tf_op jit(solution)/shard_map/attend/pallas_call | solution.py:165
  50.2 2.1 %fusion.6 = (bf16[2,2,32,4,512]{4,3,2,1,0:T(4,128)(2,1)S(1)}, bf16[2,2,32,4,512]{4,3,2,1,0:T(4,128)(2,1)S(1)}) fusion(bf16[2,2,32,8,512]{4,3,2,1,0:T(8,128)(2,1)} %bitcast.27), kind=kLoop, calls=%fused_computation.13 | loop fusion | bytes 2097152 | tf_op jit(solution)/shard_map/slice | solution.py:386
  52.2 1.3 collective-permute-start.5
  53.5 9.9 %collective-permute-start.4 = (bf16[2,2,32,4,512]{4,3,2,1,0:T(4,128)(2,1)S(1)}, bf16[2,2,32,4,512]{4,3,2,1,0:T(4,128)(2,1)S(1)}, u32[]{:S(2)}, u32[]{:S(2)}) collective-permute-start(bf16[2,2,32,4,512]{4,3,2,1,0:T(4,128)(2,1)S(1)} %get-tuple-element.40), channel_id=1, source_target_pairs={{0,1},{1,2},{2,3},{3,4},{4,5},{5,6},{6,7},{8,9},{9,10},{10,11},{11... | collective-permute-start | bytes 1572872 | tf_op jit(solution)/shard_map/ppermute | solution.py:359
  63.5 1.4 collective-permute-done.4
  64.9 3.3 %fusion.1 = (bf16[2,2,32,16,512]{4,3,2,1,0:T(8,128)(2,1)S(1)}, f32[2,2,32,16,512]{4,3,2,1,0:T(8,128)S(1)}) fusion(f32[2,2,32,16,512]{4,3,2,1,0:T(8,128)} %bitcast.23, bf16[2,2,32,4,512]{4,3,2,1,0:T(4,128)(2,1)S(1)} %collective-permute-done.5, bf16[16]{0:T(256)(128)(2,1)S(1)} %pad.4.clone, bf16[2,2,32,4,512]{4,3,2,1,0:T(4,128)(2,1)S(1)} %collective-permute-done.4), kind=kLoop, calls=%fused_computation.8 | loop fusion | flops 8388608 | bytes 11534368 | tf_op jit(solution)/shard_map/convert.1
  68.2 1.3 collective-permute-start.7
  69.5 4.6 %collective-permute-start.6 = (bf16[2,2,4,16,512]{4,3,2,1,0:T(8,128)(2,1)S(1)}, bf16[2,2,4,16,512]{4,3,2,1,0:T(8,128)(2,1)S(1)}, u32[]{:S(2)}, u32[]{:S(2)}) collective-permute-start(bf16[2,2,4,16,512]{4,3,2,1,0:T(8,128)(2,1)S(1)} %get-tuple-element.32), channel_id=1, source_target_pairs={{0,8},{8,16},{16,24},{1,9},{9,17},{17,25},{2,10},{10,18},{18,26},{... | collective-permute-start | bytes 786440 | tf_op jit(solution)/shard_map/ppermute | solution.py:359
  74.1 0.1 pad.1.clone
  74.2 2.3 %collective-permute-done.7 = bf16[2,2,4,16,512]{4,3,2,1,0:T(8,128)(2,1)S(1)} collective-permute-done((bf16[2,2,4,16,512]{4,3,2,1,0:T(8,128)(2,1)S(1)}, bf16[2,2,4,16,512]{4,3,2,1,0:T(8,128)(2,1)S(1)}, u32[]{:S(2)}, u32[]{:S(2)}) %collective-permute-start.7) | collective-permute-done | bytes 262176 | tf_op jit(solution)/shard_map/ppermute | solution.py:359
  76.5 1.5 %collective-permute-done.6 = bf16[2,2,4,16,512]{4,3,2,1,0:T(8,128)(2,1)S(1)} collective-permute-done((bf16[2,2,4,16,512]{4,3,2,1,0:T(8,128)(2,1)S(1)}, bf16[2,2,4,16,512]{4,3,2,1,0:T(8,128)(2,1)S(1)}, u32[]{:S(2)}, u32[]{:S(2)}) %collective-permute-start.6) | collective-permute-done | bytes 262176 | tf_op jit(solution)/shard_map/ppermute | solution.py:359
  78.0 0.6 fusion
  78.6 1.3 fusion.4
  79.8 8.8 %weights.1 = (bf16[768,512]{1,0:T(8,128)(2,1)}, bf16[2,8,4,64,256]{4,3,2,1,0:T(8,128)(2,1)}) custom-call(bf16[768,512]{1,0:T(8,128)(2,1)} %bitcast.28, bf16[512,768]{1,0:T(8,128)(2,1)} %get-tuple-element.18.ot_ref, bf16[768,512]{1,0:T(8,128)(2,1)} %bitcast.24, bf16[768,512]{1,0:T(8,128)(2,1)} %bitcast.20, bf16[768,512]{1,0:T(8,128)(2,1)} %bitcast.18, ...), custom_call_target="tpu_custom_call" | custom-call | tf_op jit(solution)/shard_map/weights/pallas_call | solution.py:232
  88.6 50.3 %reduce.1 = (f32[128,192]{1,0:T(8,128)}, f32[128,64]{1,0:T(8,128)}) custom-call(bf16[2,32,64,256]{3,2,1,0:T(8,128)(2,1)} %bitcast.26), custom_call_target="tpu_custom_call" | custom-call | tf_op jit(solution)/shard_map/reduce/pallas_call | solution.py:341
  138.9 1.6 %copy.12 = f32[128,192]{0,1:T(8,128)} copy(f32[128,192]{1,0:T(8,128)} %get-tuple-element.28) | data formatting | bytes 196608
  140.6 1.5 %copy.13 = f32[128,64]{0,1:T(8,128)} copy(f32[128,64]{1,0:T(8,128)} %get-tuple-element.29) | data formatting | bytes 65536
  (12 shorter events, 0.2 us)
Async XLA Ops:
  8.8 11.7 %copy-start.1 = (bf16[2,2,384,512]{3,2,1,0:T(8,128)(2,1)S(1)}, bf16[2,2,384,512]{3,2,1,0:T(8,128)(2,1)}, u32[]{:S(2)}) copy-start(bf16[2,2,384,512]{3,2,1,0:T(8,128)(2,1)} %get-tuple-element.17) | copy-start | bytes 4718596
  10.0 10.5 %collective-permute-start = (bf16[2,2,64,512]{3,2,1,0:T(8,128)(2,1)S(1)}, bf16[2,2,64,512]{3,2,1,0:T(8,128)(2,1)S(1)}, u32[]{:S(2)}, u32[]{:S(2)}) collective-permute-start(bf16[2,2,64,512]{3,2,1,0:T(8,128)(2,1)S(1)} %get-tuple-element.39), channel_id=1, source_target_pairs={{0,8},{8,16},{16,24},{1,9},{9,17},{17,25},{2,10},{10,18},{18,26},{... | collective-permute-start | bytes 786440 | tf_op jit(solution)/shard_map/ppermute | solution.py:359
  15.0 9.7 %collective-permute-start.1 = (bf16[2,2,64,512]{3,2,1,0:T(8,128)(2,1)S(1)}, bf16[2,2,64,512]{3,2,1,0:T(8,128)(2,1)S(1)}, u32[]{:S(2)}, u32[]{:S(2)}) collective-permute-start(bf16[2,2,64,512]{3,2,1,0:T(8,128)(2,1)S(1)} %get-tuple-element.38), channel_id=1, source_target_pairs={{8,0},{16,8},{24,16},{9,1},{17,9},{25,17},{10,2},{18,10},{26,18},{... | collective-permute-start | bytes 786440 | tf_op jit(solution)/shard_map/ppermute | solution.py:359
  24.6 7.8 %copy-start = (bf16[2,2,512,512]{3,2,1,0:T(8,128)(2,1)}, bf16[2,2,512,512]{3,2,1,0:T(8,128)(2,1)S(1)}, u32[]{:S(2)}) copy-start(bf16[2,2,512,512]{3,2,1,0:T(8,128)(2,1)S(1)} %constant_dynamic-update-slice_fusion.kvc_ref) | copy-start | bytes 6291460
  25.1 4.4 %collective-permute-start.3 = (bf16[2,2,32,4,512]{4,3,2,1,0:T(4,128)(2,1)S(1)}, bf16[2,2,32,4,512]{4,3,2,1,0:T(4,128)(2,1)S(1)}, u32[]{:S(2)}, u32[]{:S(2)}) collective-permute-start(bf16[2,2,32,4,512]{4,3,2,1,0:T(4,128)(2,1)S(1)} %get-tuple-element.35), channel_id=1, source_target_pairs={{1,0},{2,1},{3,2},{4,3},{5,4},{6,5},{7,6},{9,8},{10,9},{11,10},{12... | collective-permute-start | bytes 1572872 | tf_op jit(solution)/shard_map/ppermute | solution.py:359
  26.4 4.6 %collective-permute-start.2 = (bf16[2,2,32,4,512]{4,3,2,1,0:T(4,128)(2,1)S(1)}, bf16[2,2,32,4,512]{4,3,2,1,0:T(4,128)(2,1)S(1)}, u32[]{:S(2)}, u32[]{:S(2)}) collective-permute-start(bf16[2,2,32,4,512]{4,3,2,1,0:T(4,128)(2,1)S(1)} %get-tuple-element.34), channel_id=1, source_target_pairs={{0,1},{1,2},{2,3},{3,4},{4,5},{5,6},{6,7},{8,9},{9,10},{10,11},{11... | collective-permute-start | bytes 1572872 | tf_op jit(solution)/shard_map/ppermute | solution.py:359
  52.2 11.3 %collective-permute-start.5 = (bf16[2,2,32,4,512]{4,3,2,1,0:T(4,128)(2,1)S(1)}, bf16[2,2,32,4,512]{4,3,2,1,0:T(4,128)(2,1)S(1)}, u32[]{:S(2)}, u32[]{:S(2)}) collective-permute-start(bf16[2,2,32,4,512]{4,3,2,1,0:T(4,128)(2,1)S(1)} %get-tuple-element.41), channel_id=1, source_target_pairs={{1,0},{2,1},{3,2},{4,3},{5,4},{6,5},{7,6},{9,8},{10,9},{11,10},{12... | collective-permute-start | bytes 1572872 | tf_op jit(solution)/shard_map/ppermute | solution.py:359
  53.5 11.4 %collective-permute-start.4 = (bf16[2,2,32,4,512]{4,3,2,1,0:T(4,128)(2,1)S(1)}, bf16[2,2,32,4,512]{4,3,2,1,0:T(4,128)(2,1)S(1)}, u32[]{:S(2)}, u32[]{:S(2)}) collective-permute-start(bf16[2,2,32,4,512]{4,3,2,1,0:T(4,128)(2,1)S(1)} %get-tuple-element.40), channel_id=1, source_target_pairs={{0,1},{1,2},{2,3},{3,4},{4,5},{5,6},{6,7},{8,9},{9,10},{10,11},{11... | collective-permute-start | bytes 1572872 | tf_op jit(solution)/shard_map/ppermute | solution.py:359
  68.2 8.3 %collective-permute-start.7 = (bf16[2,2,4,16,512]{4,3,2,1,0:T(8,128)(2,1)S(1)}, bf16[2,2,4,16,512]{4,3,2,1,0:T(8,128)(2,1)S(1)}, u32[]{:S(2)}, u32[]{:S(2)}) collective-permute-start(bf16[2,2,4,16,512]{4,3,2,1,0:T(8,128)(2,1)S(1)} %get-tuple-element.33), channel_id=1, source_target_pairs={{8,0},{16,8},{24,16},{9,1},{17,9},{25,17},{10,2},{18,10},{26,18},{... | collective-permute-start | bytes 786440 | tf_op jit(solution)/shard_map/ppermute | solution.py:359
  69.5 8.4 %collective-permute-start.6 = (bf16[2,2,4,16,512]{4,3,2,1,0:T(8,128)(2,1)S(1)}, bf16[2,2,4,16,512]{4,3,2,1,0:T(8,128)(2,1)S(1)}, u32[]{:S(2)}, u32[]{:S(2)}) collective-permute-start(bf16[2,2,4,16,512]{4,3,2,1,0:T(8,128)(2,1)S(1)} %get-tuple-element.32), channel_id=1, source_target_pairs={{0,8},{8,16},{16,24},{1,9},{9,17},{17,25},{2,10},{10,18},{18,26},{... | collective-permute-start | bytes 786440 | tf_op jit(solution)/shard_map/ppermute | solution.py:359

commit v3 on v2

--- a/solution.py
+++ b/solution.py
@@ -71,13 +71,15 @@
     )(q, k, v, g, factors, crop_start, w_out)
 
 
-def attend_kernel(q_ref, do_ref, kvc_ref, kvs_ref, ot_ref, dq_ref, dc_ref, ds_ref, bias_ref,
-                  *, breadth, head_dim):
+def attend_kernel(q_ref, do_ref, kv_ref, rows_ref, sides_ref, ot_ref, dq_ref, own_ref,
+                  drows_ref, dsides_ref, bias_ref, *, breadth, head_dim):
     strip_cells = BLOCK * breadth
-    side_cells = BLOCK * 2 * RADIUS
-    strips = q_ref.shape[1] // strip_cells
+    rim_c = RADIUS * breadth
+    side_cells = BLOCK * RADIUS
+    cells = q_ref.shape[1]
+    strips = cells // strip_cells
     keys_c, keys_s = 2 * strip_cells, 2 * side_cells
-    keys = keys_c + keys_s
+    keys = keys_c + 2 * keys_s
     lanes = q_ref.shape[2]
     stacked = (lanes // head_dim) * strip_cells
     height = strips * BLOCK
@@ -87,11 +89,10 @@
         key = lax.broadcasted_iota(jnp.int32, (keys, stacked), 0)
         query = lax.broadcasted_iota(jnp.int32, (keys, stacked), 1) % strip_cells
         side = key - keys_c
-        key_row = jnp.where(key < keys_c, key // breadth, side // (2 * RADIUS)) - RADIUS
-        along = side % (2 * RADIUS)
+        key_row = jnp.where(key < keys_c, key // breadth, (side % keys_s) // RADIUS) - RADIUS
         key_col = jnp.where(
             key < keys_c, key % breadth,
-            jnp.where(along < RADIUS, along - RADIUS, along - RADIUS + breadth))
+            side % RADIUS + jnp.where(side < keys_s, -RADIUS, breadth))
         d_row = key_row - query // breadth
         d_col = key_col - query % breadth
         near = (jnp.abs(d_row) <= RADIUS) & (jnp.abs(d_col) <= RADIUS)
@@ -114,17 +115,39 @@
             [whole[h * head_dim:(h + 1) * head_dim, h * strip_cells:(h + 1) * strip_cells]
              for h in range(lanes // head_dim)], 0)
 
+    def keys_of(which, strip):
+        low, high = strip * strip_cells - rim_c, (strip + 2) * strip_cells - rim_c
+        parts = [kv_ref[which, 0, max(low, 0):min(high, cells)]]
+        if low < 0:
+            parts.insert(0, rows_ref[0, which, 0])
+        if high > cells:
+            parts.append(rows_ref[1, which, 0])
+        for side in range(2):
+            parts.append(sides_ref[side, which, 0, strip * side_cells:strip * side_cells + keys_s])
+        return jnp.concatenate(parts, 0)
+
+    def put(which, chunk, center, sides):
+        low = chunk * strip_cells - rim_c
+        if chunk == 0:
+            drows_ref[0, which, 0] = center[:rim_c].astype(BF16)
+            own_ref[which, 0, :strip_cells - rim_c] = center[rim_c:]
+        elif chunk == strips:
+            own_ref[which, 0, low:] = center[:cells - low]
+            drows_ref[1, which, 0] = center[cells - low:].astype(BF16)
+        else:
+            own_ref[which, 0, low:low + strip_cells] = center
+        for side in range(2):
+            dsides_ref[side, which, 0, chunk * side_cells:(chunk + 1) * side_cells] = (
+                sides[side].astype(BF16))
+
     carry = None
     for strip in range(strips):
         at = slice(strip * strip_cells, (strip + 1) * strip_cells)
-        at_c = slice(strip * strip_cells, strip * strip_cells + keys_c)
-        at_s = slice(strip * side_cells, strip * side_cells + keys_s)
         q = q_ref[0, at] * scale
         g = do_ref[0, at]
         q_stack = jnp.concatenate([q * m for m in masks], 0)
         g_stack = jnp.concatenate([g * m for m in masks], 0)
-        k = jnp.concatenate([kvc_ref[0, 0, at_c], kvs_ref[0, 0, at_s]], 0)
-        v = jnp.concatenate([kvc_ref[1, 0, at_c], kvs_ref[1, 0, at_s]], 0)
+        k, v = keys_of(0, strip), keys_of(1, strip)
         scores = dot(k, q_stack, ((1,), (1,))) + bias_ref[strip]
         weights = jnp.exp(scores - jnp.max(scores, axis=0, keepdims=True))
         softmax = weights * (1.0 / jnp.sum(weights, axis=0, keepdims=True))
@@ -136,21 +159,24 @@
         dq = by_head(dot(k, grad_scores, ((0,), (0,)))) * scale
         dq_ref[0, at] = dq.T.astype(BF16)
         parts = (dot(grad_scores, q_stack, ((1,), (0,))), dot(half, g_stack, ((1,), (0,))))
+        after = []
         for which in range(2):
-            part_c, part_s = parts[which][:keys_c], parts[which][keys_c:]
-            first_c, first_s = part_c[:strip_cells], part_s[:side_cells]
+            pieces = [parts[which][:strip_cells]]
+            rest = [parts[which][strip_cells:keys_c]]
+            for side in range(2):
+                first = keys_c + side * keys_s
+                pieces.append(parts[which][first:first + side_cells])
+                rest.append(parts[which][first + side_cells:first + keys_s])
             if carry is not None:
-                first_c = first_c + carry[which][0]
-                first_s = first_s + carry[which][1]
-            dc_ref[which, 0, at] = first_c
-            ds_ref[which, 0, strip * side_cells:(strip + 1) * side_cells] = first_s.astype(BF16)
-        carry = [(p[strip_cells:keys_c], p[keys_c + side_cells:]) for p in parts]
+                pieces = [p + c for p, c in zip(pieces, carry[which])]
+            put(which, strip, pieces[0], pieces[1:])
+            after.append(rest)
+        carry = after
     for which in range(2):
-        dc_ref[which, 0, strips * strip_cells:] = carry[which][0]
-        ds_ref[which, 0, strips * side_cells:] = carry[which][1].astype(BF16)
-
-
-def attend(q, do, kv_c, kv_s, breadth):
+        put(which, strips, carry[which][0], carry[which][1:])
+
+
+def attend(q, do, kv, rim_rows, sides, breadth):
     members, cells, features = q.shape
     head_dim = features // HEADS
     lanes = 128
@@ -160,21 +186,134 @@
     spec = pl.BlockSpec((1, cells, lanes), lambda b, h: (b, 0, h))
 
     def kv_spec(array):
-        return pl.BlockSpec((2, 1, array.shape[2], lanes), lambda b, h: (0, b, 0, h))
+        lead = array.shape[:-3]
+        return pl.BlockSpec(lead + (1, array.shape[-2], lanes),
+                            lambda b, h: (0,) * len(lead) + (b, 0, h))
 
     return pl.pallas_call(
         functools.partial(attend_kernel, breadth=breadth, head_dim=head_dim),
         grid=(members, features // lanes),
-        in_specs=[spec, spec, kv_spec(kv_c), kv_spec(kv_s)],
+        in_specs=[spec, spec, kv_spec(kv), kv_spec(rim_rows), kv_spec(sides)],
         out_specs=[pl.BlockSpec((lanes, cells), lambda b, h: (h, b)), spec,
-                   kv_spec(kv_c), kv_spec(kv_s)],
+                   kv_spec(kv), kv_spec(rim_rows), kv_spec(sides)],
         out_shape=[jax.ShapeDtypeStruct((features, members * cells), BF16),
                    jax.ShapeDtypeStruct(q.shape, BF16),
-                   jax.ShapeDtypeStruct(kv_c.shape, F32),
-                   jax.ShapeDtypeStruct(kv_s.shape, BF16)],
+                   jax.ShapeDtypeStruct(kv.shape, F32),
+                   jax.ShapeDtypeStruct(rim_rows.shape, BF16),
+                   jax.ShapeDtypeStruct(sides.shape, BF16)],
         scratch_shapes=[pltpu.VMEM((strips, keys, stacked), F32)],
         name="attend",
-    )(q, do, kv_c, kv_s)
+    )(q, do, kv, rim_rows, sides)
+
+
+DIRECTIONS = [(0, 1), (0, -1), (1, 0), (-1, 0), (1, 1), (1, -1), (-1, 1), (-1, -1)]
+
+
+def exchange_kernel(*refs, rows, cols, inputs, table):
+    arrays, (send_sem, recv_sem) = refs[:-2], refs[-2:]
+    sources, targets = arrays[:inputs], arrays[inputs:]
+    row, col = lax.axis_index("row"), lax.axis_index("col")
+
+    def present(dr, dc):
+        return ((row + dr >= 0) & (row + dr < rows) & (col + dc >= 0) & (col + dc < cols))
+
+    barrier = pltpu.get_barrier_semaphore()
+    met = 0
+    for dr, dc in DIRECTIONS:
+        there = present(dr, dc)
+
+        @pl.when(there)
+        def _(dr=dr, dc=dc):
+            pl.semaphore_signal(barrier, inc=1, device_id=(row + dr, col + dc),
+                                device_id_type=pl.DeviceIdType.MESH)
+
+        met = met + there.astype(jnp.int32)
+    pl.semaphore_wait(barrier, met)
+
+    def copy_of(at):
+        dr, dc = DIRECTIONS[at]
+        source, source_at, target, target_at = table[dr, dc]
+        return pltpu.make_async_remote_copy(
+            src_ref=sources[source].at[source_at], dst_ref=targets[target].at[target_at],
+            send_sem=send_sem.at[at], recv_sem=recv_sem.at[at],
+            device_id=(row + dr, col + dc), device_id_type=pl.DeviceIdType.MESH)
+
+    for at, (dr, dc) in enumerate(DIRECTIONS):
+        @pl.when(present(dr, dc))
+        def _(at=at):
+            copy_of(at).start()
+
+    for at, (dr, dc) in enumerate(DIRECTIONS):
+        @pl.when(jnp.logical_not(present(-dr, -dc)))
+        def _(at=at):
+            _, _, target, target_at = table[DIRECTIONS[at]]
+            view = targets[target].at[target_at]
+            view[...] = jnp.zeros(view.shape, BF16)
+
+    for at, (dr, dc) in enumerate(DIRECTIONS):
+        @pl.when(present(dr, dc))
+        def _(at=at):
+            copy_of(at).wait_send()
+
+        @pl.when(present(-dr, -dc))
+        def _(at=at):
+            copy_of(at).wait_recv()
+
+
+def exchange(arrays, shapes, table, rows, cols, collective_id, name):
+    return pl.pallas_call(
+        functools.partial(exchange_kernel, rows=rows, cols=cols, inputs=len(arrays),
+                          table=table),
+        in_specs=[pl.BlockSpec(memory_space=pl.ANY)] * len(arrays),
+        out_specs=[pl.BlockSpec(memory_space=pltpu.VMEM)] * len(shapes),
+        out_shape=[jax.ShapeDtypeStruct(shape, BF16) for shape in shapes],
+        scratch_shapes=[pltpu.SemaphoreType.DMA((8,)), pltpu.SemaphoreType.DMA((8,))],
+        compiler_params=pltpu.CompilerParams(
+            collective_id=collective_id, has_side_effects=True),
+        name=name,
+    )(*arrays)
+
+
+def span(*lead, first=0, size):
+    return lead + (slice(None), slice(None), pl.ds(first, size))
+
+
+def key_halos(kv, edges, breadth, rows, cols):
+    _, members, cells, features = kv.shape
+    rim, corner, along = RADIUS * breadth, RADIUS * RADIUS, edges.shape[3]
+    last = along - corner
+    table = {
+        (1, 0): (0, span(first=cells - rim, size=rim), 0, span(0, size=rim)),
+        (-1, 0): (0, span(size=rim), 0, span(1, size=rim)),
+        (0, 1): (1, span(1, size=along), 1, span(0, first=corner, size=along)),
+        (0, -1): (1, span(0, size=along), 1, span(1, first=corner, size=along)),
+        (1, 1): (1, span(1, first=last, size=corner), 1, span(0, size=corner)),
+        (1, -1): (1, span(0, first=last, size=corner), 1, span(1, size=corner)),
+        (-1, 1): (1, span(1, size=corner), 1, span(0, first=corner + along, size=corner)),
+        (-1, -1): (1, span(0, size=corner), 1, span(1, first=corner + along, size=corner)),
+    }
+    shapes = [(2, 2, members, rim, features), (2, 2, members, along + 2 * corner, features)]
+    return exchange([kv, edges], shapes, table, rows, cols, 2, "key_halos")
+
+
+def returned_rims(d_rows, d_sides, rows, cols):
+    _, _, members, rim, features = d_rows.shape
+    corner = RADIUS * RADIUS
+    along = d_sides.shape[3] - 2 * corner
+    end = corner + along
+    table = {
+        (1, 0): (0, span(1, size=rim), 0, span(0, size=rim)),
+        (-1, 0): (0, span(0, size=rim), 0, span(1, size=rim)),
+        (0, 1): (1, span(1, first=corner, size=along), 1, span(0, size=along)),
+        (0, -1): (1, span(0, first=corner, size=along), 1, span(1, size=along)),
+        (1, 1): (1, span(1, first=end, size=corner), 2, span(0, 0, size=corner)),
+        (1, -1): (1, span(0, first=end, size=corner), 2, span(1, 0, size=corner)),
+        (-1, 1): (1, span(1, size=corner), 2, span(0, 1, size=corner)),
+        (-1, -1): (1, span(0, size=corner), 2, span(1, 1, size=corner)),
+    }
+    shapes = [d_rows.shape, (2, 2, members, along, features),
+              (2, 2, 2, members, corner, features)]
+    return exchange([d_rows, d_sides], shapes, table, rows, cols, 3, "returned_rims")
 
 
 def bits_of(count):
@@ -244,7 +383,7 @@
     )(tokens, o_t, dq, dk, dv, g, w_qkv, dq, dk, dv)
 
 
-def reduce_kernel(buf_ref, qkv_ref, out_ref, work, recv, own_sq, all_sq,
+def reduce_kernel(buf_ref, part_ref, work, recv, own_sq, all_sq,
                   send_sem, recv_sem, sq_send, sq_recv, *, rows, cols):
     orders = halving_orders(rows, cols)
     count = rows * cols
@@ -326,10 +465,7 @@
     lax.fori_loop(1, count, send, 0)
     total = jnp.sum(lax.fori_loop(1, count, take, own_sq[...]), keepdims=True)
     factor = jnp.minimum(1.0, max_norm / jnp.sqrt(total + tiny_square))
-    part = part * factor
-    split = qkv_ref.shape[1]
-    qkv_ref[...] = part[:, :split]
-    out_ref[...] = part[:, split:]
+    part_ref[...] = part * factor
 
 
 def reduce_pieces(pieces, rows, cols):
@@ -340,9 +476,8 @@
     vmem = pl.BlockSpec(memory_space=pltpu.VMEM)
     return pl.pallas_call(
         functools.partial(reduce_kernel, rows=rows, cols=cols),
-        in_specs=[vmem], out_specs=[vmem, vmem],
-        out_shape=[jax.ShapeDtypeStruct((2 * half_rows, 3 * lanes // 4), F32),
-                   jax.ShapeDtypeStruct((2 * half_rows, lanes // 4), F32)],
+        in_specs=[vmem], out_specs=vmem,
+        out_shape=jax.ShapeDtypeStruct((2 * half_rows, lanes), F32),
         scratch_shapes=[
             pltpu.VMEM((2, count // 2, half_rows, lanes), BF16),
             pltpu.VMEM((2, count, half_rows, lanes), BF16),
@@ -371,33 +506,28 @@
 
     q, kv, g, do = prepare(flat(q_saved), flat(k_saved), flat(v_saved), flat(grad_out),
                            factors, crop_start, w_out, breadth)
-    edge = RADIUS * breadth
-    kv_c = jnp.concatenate(
-        [passed_along(kv[:, :, -edge:], "row", 1), kv,
-         passed_along(kv[:, :, :edge], "row", -1)], axis=2)
-    grid = kv_c.reshape(2, members, height + 2 * RADIUS, breadth, features)
-    kv_s = jnp.concatenate(
-        [passed_along(grid[:, :, :, -RADIUS:], "col", 1),
-         passed_along(grid[:, :, :, :RADIUS], "col", -1)], axis=3)
-    kv_s = kv_s.reshape(2, members, -1, features)
-    o_t, dq, d_c, d_s = attend(q, do, kv_c, kv_s, breadth)
-    d_c = d_c.reshape(2, members, height + 2 * RADIUS, breadth, features)
-    d_s = d_s.reshape(2, members, height + 2 * RADIUS, 2 * RADIUS, features)
-    from_left = passed_along(d_s[:, :, :, RADIUS:], "col", 1)
-    from_right = passed_along(d_s[:, :, :, :RADIUS], "col", -1)
-    gap = jnp.zeros(d_s.shape[:3] + (breadth - 2 * RADIUS, features), BF16)
-    d_c = d_c + jnp.concatenate([from_left, gap, from_right], axis=3).astype(F32)
-    from_up = passed_along(d_c[:, :, -RADIUS:].astype(BF16), "row", 1)
-    from_down = passed_along(d_c[:, :, :RADIUS].astype(BF16), "row", -1)
-    gap = jnp.zeros((2, members, height - 2 * RADIUS, breadth, features), BF16)
-    owned = d_c[:, :, RADIUS:-RADIUS] + jnp.concatenate(
-        [from_up, gap, from_down], axis=2).astype(F32)
+    grid = kv.reshape(2, members, height, breadth, features)
+    edges = jnp.stack([grid[:, :, :, :RADIUS], grid[:, :, :, -RADIUS:]])
+    edges = edges.reshape(2, 2, members, height * RADIUS, features)
+    rim_rows, sides = key_halos(kv, edges, breadth, rows, cols)
+    o_t, dq, own, d_rows, d_sides = attend(q, do, kv, rim_rows, sides, breadth)
+    rim_in, side_in, corner_in = returned_rims(d_rows, d_sides, rows, cols)
+    gap = jnp.zeros((2, 2, members, (height - 2 * RADIUS) * RADIUS, features), BF16)
+    side_in = side_in.astype(F32) + jnp.concatenate(
+        [corner_in[:, 0], gap, corner_in[:, 1]], axis=3).astype(F32)
+    side_in = side_in.reshape(2, 2, members, height, RADIUS, features)
+    gap = jnp.zeros((2, members, height, breadth - 2 * RADIUS, features), F32)
+    owned = own.reshape(grid.shape) + jnp.concatenate([side_in[0], gap, side_in[1]], axis=3)
+    gap = jnp.zeros((2, members, cells - 2 * RADIUS * breadth, features), BF16)
+    owned = owned.reshape(2, members, cells, features) + jnp.concatenate(
+        [rim_in[0], gap, rim_in[1]], axis=2).astype(F32)
     owned = owned.astype(BF16).reshape(2, members * cells, features)
     grad_tokens, pieces = weight_pieces(
         tokens.reshape(-1, features), o_t, dq.reshape(-1, features), owned[0], owned[1],
         g.reshape(-1, features), w_qkv, rows, cols)
-    grad_qkv, grad_out_w = reduce_pieces(pieces, rows, cols)
-    return grad_tokens.reshape(tokens.shape), grad_qkv, grad_out_w
+    part = reduce_pieces(pieces, rows, cols)
+    split = 3 * features // cols
+    return grad_tokens.reshape(tokens.shape), part[:, :split], part[:, split:]
 
 
 def solution(mesh):

time: 143 us -> 118 us (0.83)
  starting transfers between devices: 27.6 us -> 0 us
  Pallas kernels: 83.5 us -> 102 us
  waiting for transfers between devices: 14.9 us -> 0 us
  other arithmetic: 6.06 us -> 4.04 us
    pallas_call x0 -> x2, Pallas kernels: none -> 31.3 us  [exchange(): pl.pallas_call(functools.partial(exchange_kernel, rows=rows, cols=cols, i...]
    ppermute x8 -> x0, starting transfers between devices: 27.6 us -> none  [passed_along(): lax.ppermute(array, axis, [(i, i + by) for i in range(size) if 0 <= i + b...]
    ppermute x8 -> x0, waiting for transfers between devices: 14.9 us -> none  [passed_along(): lax.ppermute(array, axis, [(i, i + by) for i in range(size) if 0 <= i + b...]
    pallas_call x1, Pallas kernels: 50.3 us -> 37.7 us  [reduce_pieces(): pl.pallas_call(functools.partial(reduce_kernel, rows=rows, cols=cols), in...]
    another operation x1, other arithmetic: 3.26 us -> 0.98 us  [body(): edges = jnp.stack([grid[:, :, :, :RADIUS], grid[:, :, :, -RADIUS:]])]
    reshape x1 -> x0, other arithmetic: 1.49 us -> none  [body(): kv_s = kv_s.reshape(2, members, -1, features)]
    squeeze x0 -> x4, local copies, waits for them, and re-layouts: none -> 1.48 us  [the longest x1 0.99 us: body(): corner_in[:, 0]]
    add x0 -> x1, other arithmetic: none -> 1.45 us  [body(): side_in.astype(F32)]
  transfers between devices with their start and end apart: 8 -> 0, of which waited for: 6 -> 0; matrix products, arithmetic and copies ran while one was open for 0% -> 0% of each run, Pallas kernels for 0% -> 0%
where the time goes in v3:
time: 118 us
  Pallas kernels  102 us (86%)
  local copies, waits for them, and re-layouts  10.6 us (9%)
  other arithmetic  4.04 us (3%)
    pallas_call x1, Pallas kernels, reduce_pieces(): pl.pallas_call(functools.partial(reduce_kernel, rows=rows, cols=cols), in...  37.7 us
    pallas_call x2, Pallas kernels, exchange(): pl.pallas_call(functools.partial(exchange_kernel, rows=rows, cols=cols, i...  31.3 us
    pallas_call x1, Pallas kernels, attend(): pl.pallas_call(functools.partial(attend_kernel, breadth=breadth, head_dim...  17.9 us
    pallas_call x1, Pallas kernels, weight_pieces(): pl.pallas_call(functools.partial(weights_kernel, orders=orders, rows=rows...  8.68 us
    pallas_call x1, Pallas kernels, prepare(): pl.pallas_call(functools.partial(prepare_kernel, breadth=breadth), grid=(...  6.61 us
    unnamed x6, local copies, waits for them, and re-layouts  3.77 us

profile of v3, /device:TPU:0, one launch (start us, length us, event | category | flops | bytes accessed | tf_op | source)
XLA Modules:
  0.0 117.6 jit_solution(4006174919496240082)
XLA Ops:
  0.6 0.7 multiply_exponential_fusion
  1.3 0.1 broadcast_in_dim.12
  1.4 0.8 reshape.62.fac_ref
  2.2 6.6 %prepare.1 = (bf16[2,384,512]{2,1,0:T(8,128)(2,1)}, bf16[2,2,384,512]{3,2,1,0:T(8,128)(2,1)}, bf16[2,384,512]{2,1,0:T(8,128)(2,1)}, bf16[2,384,512]{2,1,0:T(8,128)(2,1)}) custom-call(bf16[2,384,512]{2,1,0:T(8,128)(2,1)} %bitcast.44, bf16[2,384,512]{2,1,0:T(8,128)(2,1)} %bitcast.45, bf16[2,384,512]{2,1,0:T(8,128)(2,1)} %bitcast.46, ...), custom_call_target="tpu_custom_call" | custom-call | tf_op jit(solution)/shard_map/prepare/pallas_call | solution.py:61
  8.8 1.7 %fusion.4 = (bf16[2,2,24,4,512]{4,3,2,1,0:T(4,128)(2,1)S(1)}, bf16[2,2,24,4,512]{4,3,2,1,0:T(4,128)(2,1)S(1)}) fusion(bf16[2,2,24,16,512]{4,3,2,1,0:T(8,128)(2,1)} %bitcast.33), kind=kLoop, calls=%fused_computation.13 | loop fusion | bytes 1572864 | tf_op jit(solution)/shard_map/slice | solution.py:510
  10.5 0.1 stack.10
  10.6 0.1 stack.9
  10.7 1.0 pad_maximum_fusion.1.refs_1_
  11.7 15.4 %key_halos.1 = (bf16[2,2,2,64,512]{4,3,2,1,0:T(8,128)(2,1)}, bf16[2,2,2,128,512]{4,3,2,1,0:T(8,128)(2,1)}) custom-call(bf16[2,2,384,512]{3,2,1,0:T(8,128)(2,1)} %get-tuple-element.21.refs_0_.kv_ref, bf16[2,2,2,96,512]{4,3,2,1,0:T(8,128)(2,1)} %pad_maximum_fusion.1.refs_1_), custom_call_target="tpu_custom_call" | custom-call | tf_op jit(solution)/shard_map/key_halos/pallas_call | solution.py:264
  27.1 17.9 %attend.1 = (bf16[512,768]{1,0:T(8,128)(2,1)}, bf16[2,384,512]{2,1,0:T(8,128)(2,1)}, f32[2,2,384,512]{3,2,1,0:T(8,128)}, bf16[2,2,2,64,512]{4,3,2,1,0:T(8,128)(2,1)}, bf16[2,2,2,128,512]{4,3,2,1,0:T(8,128)(2,1)}) custom-call(bf16[2,384,512]{2,1,0:T(8,128)(2,1)} %get-tuple-element.19.q_ref, bf16[2,384,512]{2,1,0:T(8,128)(2,1)} %get-tuple-element.20.do_ref, ...), custom_call_target="tpu_custom_call" | custom-call | tf_op jit(solution)/shard_map/attend/pallas_call | solution.py:193
  45.1 15.9 %returned_rims.1 = (bf16[2,2,2,64,512]{4,3,2,1,0:T(8,128)(2,1)}, bf16[2,2,2,96,512]{4,3,2,1,0:T(8,128)(2,1)}, bf16[2,2,2,2,16,512]{5,4,3,2,1,0:T(8,128)(2,1)}) custom-call(bf16[2,2,2,64,512]{4,3,2,1,0:T(8,128)(2,1)} %get-tuple-element.27.refs_0_, bf16[2,2,2,128,512]{4,3,2,1,0:T(8,128)(2,1)} %get-tuple-element.28.refs_1_), custom_call_target="tpu_custom_call" | custom-call | tf_op jit(solution)/shard_map/returned_rims/pallas_call | solution.py:264
  60.9 1.0 slice_bitcast_fusion.3
  61.9 0.1 pad.7.clone
  62.0 1.4 %convert_add_fusion = f32[2,2,2,96,512]{4,3,2,1,0:T(8,128)S(1)} fusion(bf16[2,2,2,96,512]{4,3,2,1,0:T(8,128)(2,1)} %get-tuple-element.29, bf16[2,2,2,16,512]{4,3,2,1,0:T(8,128)(2,1)S(1)} %get-tuple-element.47, bf16[2,2,2,16,512]{4,3,2,1,0:T(8,128)(2,1)S(1)} %get-tuple-element.46, bf16[96]{0:T(256)(128)(2,1)S(1)} %pad.7.clone), kind=kLoop, calls=%fused_computation.4 | loop fusion | flops 3145728 | bytes 2621632 | tf_op jit(solution)/shard_map/add | solution.py:516
  63.5 0.2 fusion.3
  63.6 0.2 squeeze.26
  63.9 0.2 squeeze.27
  64.1 0.1 pad.4.clone
  64.2 0.0 copy-start.1
  64.2 0.0 copy-start
  64.2 0.5 pad_maximum_fusion
  64.7 0.5 copy-done.1
  65.3 0.1 pad.1.clone
  65.4 0.9 copy-done
  66.3 0.4 fusion.1
  66.7 1.3 %fusion.2 = (bf16[1,2,384,512]{3,2,1,0:T(8,128)(2,1)}, bf16[1,2,384,512]{3,2,1,0:T(8,128)(2,1)}) fusion(bf16[2,2,384,512]{3,2,1,0:T(8,128)(2,1)S(1)} %fusion.1), kind=kLoop, calls=%fused_computation.11 | loop fusion | bytes 3145728 | tf_op jit(solution)/shard_map/slice | solution.py:526
  67.9 8.7 %weights.1 = (bf16[768,512]{1,0:T(8,128)(2,1)}, bf16[2,8,4,64,256]{4,3,2,1,0:T(8,128)(2,1)}) custom-call(bf16[768,512]{1,0:T(8,128)(2,1)} %bitcast.42, bf16[512,768]{1,0:T(8,128)(2,1)} %get-tuple-element.24.ot_ref, bf16[768,512]{1,0:T(8,128)(2,1)} %bitcast.38, bf16[768,512]{1,0:T(8,128)(2,1)} %bitcast.36, bf16[768,512]{1,0:T(8,128)(2,1)} %bitcast.34, ...), custom_call_target="tpu_custom_call" | custom-call | tf_op jit(solution)/shard_map/weights/pallas_call | solution.py:371
  76.6 37.7 %reduce.1 = f32[128,256]{1,0:T(8,128)} custom-call(bf16[2,32,64,256]{3,2,1,0:T(8,128)(2,1)} %bitcast.40), custom_call_target="tpu_custom_call" | custom-call | tf_op jit(solution)/shard_map/reduce/pallas_call | solution.py:477
  114.3 1.6 %copy.12 = f32[128,192]{0,1:T(8,128)} copy(f32[128,192]{1,0:T(8,128)} %bitcast.41) | data formatting | bytes 196608
  115.9 0.9 slice.51
  116.9 0.7 copy.13
  (4 shorter events, 0.0 us)
Async XLA Ops:
  64.2 1.0 copy-start.1
  64.2 2.1 %copy-start = (f32[2,2,384,512]{3,2,1,0:T(8,128)S(1)}, f32[2,2,384,512]{3,2,1,0:T(8,128)}, u32[]{:S(2)}) copy-start(f32[2,2,384,512]{3,2,1,0:T(8,128)} %get-tuple-element.26) | copy-start | bytes 9437188

commit v4 on v3

--- a/solution.py
+++ b/solution.py
@@ -11,6 +11,7 @@
 HEADS = 8
 RADIUS = 4
 BLOCK = 8
+PARTS = 4
 
 max_norm = 1000.0
 masked_score = -1e30
@@ -321,39 +322,35 @@
 
 
 def halving_orders(rows, cols):
-    col = [("col", k) for k in range(bits_of(cols))]
-    row = [("row", k) for k in range(bits_of(rows))]
-    return [col[:1] + col[1:] + row, col[:1] + col[:0:-1] + row]
-
-
-def col_place(order, col):
+    bits = [("col", k) for k in range(bits_of(cols))] + [("row", k) for k in range(bits_of(rows))]
+    return [bits[k:] + bits[:k] for k in range(PARTS)]
+
+
+def place_of(order, row, col):
     place = 0
     for axis, bit in order:
-        if axis == "col":
-            place = 2 * place + (col >> bit) % 2
+        place = 2 * place + ((row if axis == "row" else col) // 2 ** bit) % 2
     return place
 
 
 def weights_kernel(tok_ref, ot_ref, dq_ref, dk_ref, dv_ref, g_ref, w_ref,
-                   dq_rows, dk_rows, dv_rows, gt_ref, buf_ref, *, orders, rows, cols):
+                   dq_rows, dk_rows, dv_rows, gt_ref, buf_ref, *, orders, cols):
     features = g_ref.shape[1]
     tok = tok_ref[...]
     raw = jnp.concatenate(
         [dot(tok, ref[...], ((0,), (0,))) for ref in (dq_ref, dk_ref, dv_ref)], 1)
     raw_out = dot(ot_ref[...], g_ref[...], ((1,), (0,)))
     wide, narrow = 3 * features // cols, features // cols
-    part_rows = buf_ref.shape[3]
-    group = tok.shape[1] // (2 * part_rows)
-    nbits = bits_of(rows)
+    part_rows = buf_ref.shape[2]
+    group = tok.shape[1] // (PARTS * part_rows)
     for member, col in ((m, c) for m in range(group) for c in range(cols)):
         row = pl.program_id(0) * group + member
-        place = sum(((row // 2 ** k) % 2) * 2 ** (nbits - 1 - k) for k in range(nbits))
         piece = jnp.concatenate(
             [raw[:, col * wide:(col + 1) * wide], raw_out[:, col * narrow:(col + 1) * narrow]],
             1).astype(BF16)
         for half, order in enumerate(orders):
-            first = (2 * member + half) * part_rows
-            buf_ref[half, col_place(order, col), place] = piece[first:first + part_rows]
+            first = (PARTS * member + half) * part_rows
+            buf_ref[half, place_of(order, row, col)] = piece[first:first + part_rows]
     total = dot(dq_rows[...], w_ref[:, :features], ((1,), (1,)))
     total = total + dot(dk_rows[...], w_ref[:, features:2 * features], ((1,), (1,)))
     total = total + dot(dv_rows[...], w_ref[:, 2 * features:], ((1,), (1,)))
@@ -369,16 +366,16 @@
     some = pl.BlockSpec((cells * group // rows, features), lambda r: (r, 0))
     lanes = 4 * features // cols
     return pl.pallas_call(
-        functools.partial(weights_kernel, orders=orders, rows=rows, cols=cols),
+        functools.partial(weights_kernel, orders=orders, cols=cols),
         grid=(rows // group,),
         in_specs=[pl.BlockSpec((cells, group * part_rows), lambda r: (0, r)),
                   pl.BlockSpec((group * part_rows, cells), lambda r: (r, 0)),
                   whole, whole, whole, whole,
                   pl.BlockSpec(w_qkv.shape, lambda r: (0, 0)), some, some, some],
-        out_specs=[some, pl.BlockSpec((2, cols, rows, part_rows // 2, lanes),
-                                      lambda r: (0, 0, 0, 0, 0))],
+        out_specs=[some, pl.BlockSpec((PARTS, rows * cols, part_rows // PARTS, lanes),
+                                      lambda r: (0, 0, 0, 0))],
         out_shape=[jax.ShapeDtypeStruct((cells, features), BF16),
-                   jax.ShapeDtypeStruct((2, cols, rows, part_rows // 2, lanes), BF16)],
+                   jax.ShapeDtypeStruct((PARTS, rows * cols, part_rows // PARTS, lanes), BF16)],
         name="weights",
     )(tokens, o_t, dq, dk, dv, g, w_qkv, dq, dk, dv)
 
@@ -404,8 +401,8 @@
     lax.fori_loop(1, count, greet, 0)
     pl.semaphore_wait(barrier, count - 1)
     steps = len(orders[0])
-    base = [0, 0]
-    finals = [None, None]
+    base = [0] * PARTS
+    finals = [None] * PARTS
 
     def start(half, step):
         axis, bit = orders[half][step]
@@ -423,9 +420,9 @@
         copy.start()
         return copy, size, mybit
 
-    flights = [start(half, 0) for half in range(2)]
+    flights = [start(half, 0) for half in range(PARTS)]
     for step in range(steps):
-        for half in range(2):
+        for half in range(PARTS):
             copy, size, mybit = flights[half]
             copy.wait()
             keep = base[half] + mybit * size
@@ -436,12 +433,8 @@
             source = buf_ref if step == 0 else work
             base[half] = 0 if step == 0 else keep
 
-            def add(i, _, half=half, keep=keep, first=first, source=source, to=base[half]):
-                work[half, to + i] = (source[half, keep + i].astype(F32)
-                                      + recv[half, first + i].astype(F32)).astype(BF16)
-                return 0
-
-            lax.fori_loop(0, size, add, 0)
+            work[half, pl.ds(base[half], size)] = (
+                source[half, pl.ds(keep, size)] + recv[half, pl.ds(first, size)])
             flights[half] = start(half, step + 1)
     part = jnp.concatenate(finals, 0)
     squares = jnp.sum((part * part).reshape(-1, 8, part.shape[1]), axis=0)
@@ -470,19 +463,19 @@
 
 def reduce_pieces(pieces, rows, cols):
     count = rows * cols
-    half_rows, lanes = pieces.shape[3:]
-    pieces = pieces.reshape(2, count, half_rows, lanes)
+    half_rows, lanes = pieces.shape[2:]
     steps = bits_of(count)
     vmem = pl.BlockSpec(memory_space=pltpu.VMEM)
     return pl.pallas_call(
         functools.partial(reduce_kernel, rows=rows, cols=cols),
         in_specs=[vmem], out_specs=vmem,
-        out_shape=jax.ShapeDtypeStruct((2 * half_rows, lanes), F32),
+        out_shape=jax.ShapeDtypeStruct((PARTS * half_rows, lanes), F32),
         scratch_shapes=[
-            pltpu.VMEM((2, count // 2, half_rows, lanes), BF16),
-            pltpu.VMEM((2, count, half_rows, lanes), BF16),
+            pltpu.VMEM((PARTS, count // 2, half_rows, lanes), BF16),
+            pltpu.VMEM((PARTS, count, half_rows, lanes), BF16),
             pltpu.VMEM((8, 128), F32), pltpu.VMEM((count, 8, 128), F32),
-            pltpu.SemaphoreType.DMA((2, steps)), pltpu.SemaphoreType.DMA((2, steps)),
+            pltpu.SemaphoreType.DMA((PARTS, steps)),
+            pltpu.SemaphoreType.DMA((PARTS, steps)),
             pltpu.SemaphoreType.DMA((count,)), pltpu.SemaphoreType.DMA((count,))],
         compiler_params=pltpu.CompilerParams(collective_id=1, has_side_effects=True),
         name="reduce",

time: 118 us -> 121 us (1.025)
  Pallas kernels: 102 us -> 105 us
    pallas_call x1, Pallas kernels: 37.7 us -> 40.8 us  [reduce_pieces(): pl.pallas_call(functools.partial(reduce_kernel, rows=rows, cols=cols), in...]
where the time goes in v4:
time: 121 us
  Pallas kernels  105 us (87%)
  local copies, waits for them, and re-layouts  10.6 us (9%)
  other arithmetic  4.04 us (3%)
    pallas_call x1, Pallas kernels, reduce_pieces(): pl.pallas_call(functools.partial(reduce_kernel, rows=rows, cols=cols), in...  40.8 us
    pallas_call x2, Pallas kernels, exchange(): pl.pallas_call(functools.partial(exchange_kernel, rows=rows, cols=cols, i...  31.3 us
    pallas_call x1, Pallas kernels, attend(): pl.pallas_call(functools.partial(attend_kernel, breadth=breadth, head_dim...  17.9 us
    pallas_call x1, Pallas kernels, weight_pieces(): pl.pallas_call(functools.partial(weights_kernel, orders=orders, cols=cols...  8.8 us
    pallas_call x1, Pallas kernels, prepare(): pl.pallas_call(functools.partial(prepare_kernel, breadth=breadth), grid=(...  6.61 us
    unnamed x6, local copies, waits for them, and re-layouts  3.77 us

profile of v4, /device:TPU:0, one launch (start us, length us, event | category | flops | bytes accessed | tf_op | source)
XLA Modules:
  0.0 120.8 jit_solution(2412869165145366929)
XLA Ops:
  0.6 0.7 multiply_exponential_fusion
  1.3 0.1 broadcast_in_dim.12
  1.4 0.8 reshape.59.fac_ref
  2.2 6.6 %prepare.1 = (bf16[2,384,512]{2,1,0:T(8,128)(2,1)}, bf16[2,2,384,512]{3,2,1,0:T(8,128)(2,1)}, bf16[2,384,512]{2,1,0:T(8,128)(2,1)}, bf16[2,384,512]{2,1,0:T(8,128)(2,1)}) custom-call(bf16[2,384,512]{2,1,0:T(8,128)(2,1)} %bitcast.42, bf16[2,384,512]{2,1,0:T(8,128)(2,1)} %bitcast.43, bf16[2,384,512]{2,1,0:T(8,128)(2,1)} %bitcast.44, ...), custom_call_target="tpu_custom_call" | custom-call | tf_op jit(solution)/shard_map/prepare/pallas_call | solution.py:62
  8.8 1.7 %fusion.4 = (bf16[2,2,24,4,512]{4,3,2,1,0:T(4,128)(2,1)S(1)}, bf16[2,2,24,4,512]{4,3,2,1,0:T(4,128)(2,1)S(1)}) fusion(bf16[2,2,24,16,512]{4,3,2,1,0:T(8,128)(2,1)} %bitcast.32), kind=kLoop, calls=%fused_computation.13 | loop fusion | bytes 1572864 | tf_op jit(solution)/shard_map/slice | solution.py:503
  10.5 0.1 stack.10
  10.6 0.1 stack.9
  10.7 1.0 pad_maximum_fusion.1.refs_1_
  11.7 15.4 %key_halos.1 = (bf16[2,2,2,64,512]{4,3,2,1,0:T(8,128)(2,1)}, bf16[2,2,2,128,512]{4,3,2,1,0:T(8,128)(2,1)}) custom-call(bf16[2,2,384,512]{3,2,1,0:T(8,128)(2,1)} %get-tuple-element.21.refs_0_.kv_ref, bf16[2,2,2,96,512]{4,3,2,1,0:T(8,128)(2,1)} %pad_maximum_fusion.1.refs_1_), custom_call_target="tpu_custom_call" | custom-call | tf_op jit(solution)/shard_map/key_halos/pallas_call | solution.py:265
  27.1 17.9 %attend.1 = (bf16[512,768]{1,0:T(8,128)(2,1)}, bf16[2,384,512]{2,1,0:T(8,128)(2,1)}, f32[2,2,384,512]{3,2,1,0:T(8,128)}, bf16[2,2,2,64,512]{4,3,2,1,0:T(8,128)(2,1)}, bf16[2,2,2,128,512]{4,3,2,1,0:T(8,128)(2,1)}) custom-call(bf16[2,384,512]{2,1,0:T(8,128)(2,1)} %get-tuple-element.19.q_ref, bf16[2,384,512]{2,1,0:T(8,128)(2,1)} %get-tuple-element.20.do_ref, ...), custom_call_target="tpu_custom_call" | custom-call | tf_op jit(solution)/shard_map/attend/pallas_call | solution.py:194
  45.1 15.9 %returned_rims.1 = (bf16[2,2,2,64,512]{4,3,2,1,0:T(8,128)(2,1)}, bf16[2,2,2,96,512]{4,3,2,1,0:T(8,128)(2,1)}, bf16[2,2,2,2,16,512]{5,4,3,2,1,0:T(8,128)(2,1)}) custom-call(bf16[2,2,2,64,512]{4,3,2,1,0:T(8,128)(2,1)} %get-tuple-element.27.refs_0_, bf16[2,2,2,128,512]{4,3,2,1,0:T(8,128)(2,1)} %get-tuple-element.28.refs_1_), custom_call_target="tpu_custom_call" | custom-call | tf_op jit(solution)/shard_map/returned_rims/pallas_call | solution.py:265
  60.9 1.0 slice_bitcast_fusion.3
  61.9 0.1 pad.7.clone
  62.0 1.4 %convert_add_fusion = f32[2,2,2,96,512]{4,3,2,1,0:T(8,128)S(1)} fusion(bf16[2,2,2,96,512]{4,3,2,1,0:T(8,128)(2,1)} %get-tuple-element.29, bf16[2,2,2,16,512]{4,3,2,1,0:T(8,128)(2,1)S(1)} %get-tuple-element.47, bf16[2,2,2,16,512]{4,3,2,1,0:T(8,128)(2,1)S(1)} %get-tuple-element.46, bf16[96]{0:T(256)(128)(2,1)S(1)} %pad.7.clone), kind=kLoop, calls=%fused_computation.4 | loop fusion | flops 3145728 | bytes 2621632 | tf_op jit(solution)/shard_map/add | solution.py:509
  63.5 0.2 fusion.3
  63.6 0.2 squeeze.26
  63.9 0.2 squeeze.27
  64.1 0.1 pad.4.clone
  64.2 0.0 copy-start.1
  64.2 0.0 copy-start
  64.2 0.5 pad_maximum_fusion
  64.7 0.5 copy-done.1
  65.3 0.1 pad.1.clone
  65.4 0.9 copy-done
  66.3 0.4 fusion.1
  66.7 1.3 %fusion.2 = (bf16[1,2,384,512]{3,2,1,0:T(8,128)(2,1)}, bf16[1,2,384,512]{3,2,1,0:T(8,128)(2,1)}) fusion(bf16[2,2,384,512]{3,2,1,0:T(8,128)(2,1)S(1)} %fusion.1), kind=kLoop, calls=%fused_computation.11 | loop fusion | bytes 3145728 | tf_op jit(solution)/shard_map/slice | solution.py:519
  67.9 8.8 %weights.1 = (bf16[768,512]{1,0:T(8,128)(2,1)}, bf16[4,32,32,256]{3,2,1,0:T(8,128)(2,1)}) custom-call(bf16[768,512]{1,0:T(8,128)(2,1)} %bitcast.40, bf16[512,768]{1,0:T(8,128)(2,1)} %get-tuple-element.24.ot_ref, bf16[768,512]{1,0:T(8,128)(2,1)} %bitcast.37, bf16[768,512]{1,0:T(8,128)(2,1)} %bitcast.35, bf16[768,512]{1,0:T(8,128)(2,1)} %bitcast.33, ...), custom_call_target="tpu_custom_call" | custom-call | tf_op jit(solution)/shard_map/weights/pallas_call | solution.py:368
  76.7 40.8 %reduce.1 = f32[128,256]{1,0:T(8,128)} custom-call(bf16[4,32,32,256]{3,2,1,0:T(8,128)(2,1)} %get-tuple-element.34.buf_ref), custom_call_target="tpu_custom_call" | custom-call | tf_op jit(solution)/shard_map/reduce/pallas_call | solution.py:469
  117.6 1.6 %copy.12 = f32[128,192]{0,1:T(8,128)} copy(f32[128,192]{1,0:T(8,128)} %bitcast.39) | data formatting | bytes 196608
  119.2 0.9 slice.51
  120.1 0.7 copy.13
  (4 shorter events, 0.0 us)
Async XLA Ops:
  64.2 1.0 copy-start.1
  64.2 2.1 %copy-start = (f32[2,2,384,512]{3,2,1,0:T(8,128)S(1)}, f32[2,2,384,512]{3,2,1,0:T(8,128)}, u32[]{:S(2)}) copy-start(f32[2,2,384,512]{3,2,1,0:T(8,128)} %get-tuple-element.26) | copy-start | bytes 9437188

commit v5 on v4

--- a/solution.py
+++ b/solution.py
@@ -11,7 +11,7 @@
 HEADS = 8
 RADIUS = 4
 BLOCK = 8
-PARTS = 4
+PARTS = 2
 
 max_norm = 1000.0
 masked_score = -1e30
@@ -322,8 +322,9 @@
 
 
 def halving_orders(rows, cols):
-    bits = [("col", k) for k in range(bits_of(cols))] + [("row", k) for k in range(bits_of(rows))]
-    return [bits[k:] + bits[:k] for k in range(PARTS)]
+    col = [("col", k) for k in range(bits_of(cols))]
+    row = [("row", k) for k in range(bits_of(rows))]
+    return [col[:1] + col[1:] + row, col[:1] + col[:0:-1] + row]
 
 
 def place_of(order, row, col):
@@ -458,7 +459,7 @@
     lax.fori_loop(1, count, send, 0)
     total = jnp.sum(lax.fori_loop(1, count, take, own_sq[...]), keepdims=True)
     factor = jnp.minimum(1.0, max_norm / jnp.sqrt(total + tiny_square))
-    part_ref[...] = part * factor
+    part_ref[...] = (part * factor).T
 
 
 def reduce_pieces(pieces, rows, cols):
@@ -469,7 +470,7 @@
     return pl.pallas_call(
         functools.partial(reduce_kernel, rows=rows, cols=cols),
         in_specs=[vmem], out_specs=vmem,
-        out_shape=jax.ShapeDtypeStruct((PARTS * half_rows, lanes), F32),
+        out_shape=jax.ShapeDtypeStruct((lanes, PARTS * half_rows), F32),
         scratch_shapes=[
             pltpu.VMEM((PARTS, count // 2, half_rows, lanes), BF16),
             pltpu.VMEM((PARTS, count, half_rows, lanes), BF16),
@@ -520,7 +521,7 @@
         g.reshape(-1, features), w_qkv, rows, cols)
     part = reduce_pieces(pieces, rows, cols)
     split = 3 * features // cols
-    return grad_tokens.reshape(tokens.shape), part[:, :split], part[:, split:]
+    return grad_tokens.reshape(tokens.shape), part[:split].T, part[split:].T
 
 
 def solution(mesh):

time: 121 us -> 118 us (0.975)
  Pallas kernels: 105 us -> 102 us
    pallas_call x1, Pallas kernels: 40.8 us -> 37.5 us  [reduce_pieces(): pl.pallas_call(functools.partial(reduce_kernel, rows=rows, cols=cols), in...]
    transpose x0 -> x2, local copies, waits for them, and re-layouts: none -> 2.91 us  [body(): return (grad_tokens.reshape(tokens.shape), part[:split].T, part[split:].T)]
    unnamed x6 -> x4, local copies, waits for them, and re-layouts: 3.77 us -> 1.4 us
where the time goes in v5:
time: 118 us; the launch traced here: 117 us
  Pallas kernels  102 us (86%)
  local copies, waits for them, and re-layouts  10.2 us (9%)
  other arithmetic  4.04 us (3%)
    pallas_call x1, Pallas kernels, reduce_pieces(): pl.pallas_call(functools.partial(reduce_kernel, rows=rows, cols=cols), in...  37.5 us
    pallas_call x2, Pallas kernels, exchange(): pl.pallas_call(functools.partial(exchange_kernel, rows=rows, cols=cols, i...  31.3 us
    pallas_call x1, Pallas kernels, attend(): pl.pallas_call(functools.partial(attend_kernel, breadth=breadth, head_dim...  17.9 us
    pallas_call x1, Pallas kernels, weight_pieces(): pl.pallas_call(functools.partial(weights_kernel, orders=orders, cols=cols...  8.68 us
    pallas_call x1, Pallas kernels, prepare(): pl.pallas_call(functools.partial(prepare_kernel, breadth=breadth), grid=(...  6.61 us
    transpose x2, local copies, waits for them, and re-layouts, body(): return (grad_tokens.reshape(tokens.shape), part[:split].T, part[split:].T)  2.91 us

profile of v5, /device:TPU:0, one launch (start us, length us, event | category | flops | bytes accessed | tf_op | source)
XLA Modules:
  0.0 117.0 jit_solution(13996482903314107905)
XLA Ops:
  0.6 0.7 multiply_exponential_fusion
  1.3 0.1 broadcast_in_dim.12
  1.4 0.8 reshape.59.fac_ref
  2.2 6.6 %prepare.1 = (bf16[2,384,512]{2,1,0:T(8,128)(2,1)}, bf16[2,2,384,512]{3,2,1,0:T(8,128)(2,1)}, bf16[2,384,512]{2,1,0:T(8,128)(2,1)}, bf16[2,384,512]{2,1,0:T(8,128)(2,1)}) custom-call(bf16[2,384,512]{2,1,0:T(8,128)(2,1)} %bitcast.44, bf16[2,384,512]{2,1,0:T(8,128)(2,1)} %bitcast.45, bf16[2,384,512]{2,1,0:T(8,128)(2,1)} %bitcast.46, ...), custom_call_target="tpu_custom_call" | custom-call | tf_op jit(solution)/shard_map/prepare/pallas_call | solution.py:62
  8.8 1.7 %fusion.4 = (bf16[2,2,24,4,512]{4,3,2,1,0:T(4,128)(2,1)S(1)}, bf16[2,2,24,4,512]{4,3,2,1,0:T(4,128)(2,1)S(1)}) fusion(bf16[2,2,24,16,512]{4,3,2,1,0:T(8,128)(2,1)} %bitcast.35), kind=kLoop, calls=%fused_computation.15 | loop fusion | bytes 1572864 | tf_op jit(solution)/shard_map/slice | solution.py:504
  10.5 0.1 stack.10
  10.6 0.1 stack.9
  10.7 1.0 pad_maximum_fusion.1.refs_1_
  11.7 15.4 %key_halos.1 = (bf16[2,2,2,64,512]{4,3,2,1,0:T(8,128)(2,1)}, bf16[2,2,2,128,512]{4,3,2,1,0:T(8,128)(2,1)}) custom-call(bf16[2,2,384,512]{3,2,1,0:T(8,128)(2,1)} %get-tuple-element.21.refs_0_.kv_ref, bf16[2,2,2,96,512]{4,3,2,1,0:T(8,128)(2,1)} %pad_maximum_fusion.1.refs_1_), custom_call_target="tpu_custom_call" | custom-call | tf_op jit(solution)/shard_map/key_halos/pallas_call | solution.py:265
  27.1 17.9 %attend.1 = (bf16[512,768]{1,0:T(8,128)(2,1)}, bf16[2,384,512]{2,1,0:T(8,128)(2,1)}, f32[2,2,384,512]{3,2,1,0:T(8,128)}, bf16[2,2,2,64,512]{4,3,2,1,0:T(8,128)(2,1)}, bf16[2,2,2,128,512]{4,3,2,1,0:T(8,128)(2,1)}) custom-call(bf16[2,384,512]{2,1,0:T(8,128)(2,1)} %get-tuple-element.19.q_ref, bf16[2,384,512]{2,1,0:T(8,128)(2,1)} %get-tuple-element.20.do_ref, ...), custom_call_target="tpu_custom_call" | custom-call | tf_op jit(solution)/shard_map/attend/pallas_call | solution.py:194
  45.1 15.9 %returned_rims.1 = (bf16[2,2,2,64,512]{4,3,2,1,0:T(8,128)(2,1)}, bf16[2,2,2,96,512]{4,3,2,1,0:T(8,128)(2,1)}, bf16[2,2,2,2,16,512]{5,4,3,2,1,0:T(8,128)(2,1)}) custom-call(bf16[2,2,2,64,512]{4,3,2,1,0:T(8,128)(2,1)} %get-tuple-element.27.refs_0_, bf16[2,2,2,128,512]{4,3,2,1,0:T(8,128)(2,1)} %get-tuple-element.28.refs_1_), custom_call_target="tpu_custom_call" | custom-call | tf_op jit(solution)/shard_map/returned_rims/pallas_call | solution.py:265
  60.9 1.0 slice_bitcast_fusion.3
  61.9 0.1 pad.7.clone
  62.0 1.4 %convert_add_fusion = f32[2,2,2,96,512]{4,3,2,1,0:T(8,128)S(1)} fusion(bf16[2,2,2,96,512]{4,3,2,1,0:T(8,128)(2,1)} %get-tuple-element.29, bf16[2,2,2,16,512]{4,3,2,1,0:T(8,128)(2,1)S(1)} %get-tuple-element.44, bf16[2,2,2,16,512]{4,3,2,1,0:T(8,128)(2,1)S(1)} %get-tuple-element.43, bf16[96]{0:T(256)(128)(2,1)S(1)} %pad.7.clone), kind=kLoop, calls=%fused_computation.4 | loop fusion | flops 3145728 | bytes 2621632 | tf_op jit(solution)/shard_map/add | solution.py:510
  63.5 0.2 fusion.3
  63.6 0.2 squeeze.26
  63.9 0.2 squeeze.27
  64.1 0.1 pad.4.clone
  64.2 0.0 copy-start.1
  64.2 0.0 copy-start
  64.2 0.5 pad_maximum_fusion
  64.7 0.5 copy-done.1
  65.3 0.1 pad.1.clone
  65.4 0.9 copy-done
  66.3 0.4 fusion.1
  66.7 1.3 %fusion.2 = (bf16[1,2,384,512]{3,2,1,0:T(8,128)(2,1)}, bf16[1,2,384,512]{3,2,1,0:T(8,128)(2,1)}) fusion(bf16[2,2,384,512]{3,2,1,0:T(8,128)(2,1)S(1)} %fusion.1), kind=kLoop, calls=%fused_computation.13 | loop fusion | bytes 3145728 | tf_op jit(solution)/shard_map/slice | solution.py:520
  67.9 8.7 %weights.1 = (bf16[768,512]{1,0:T(8,128)(2,1)}, bf16[2,32,64,256]{3,2,1,0:T(8,128)(2,1)}) custom-call(bf16[768,512]{1,0:T(8,128)(2,1)} %bitcast.42, bf16[512,768]{1,0:T(8,128)(2,1)} %get-tuple-element.24.ot_ref, bf16[768,512]{1,0:T(8,128)(2,1)} %bitcast.40, bf16[768,512]{1,0:T(8,128)(2,1)} %bitcast.38, bf16[768,512]{1,0:T(8,128)(2,1)} %bitcast.36, ...), custom_call_target="tpu_custom_call" | custom-call | tf_op jit(solution)/shard_map/weights/pallas_call | solution.py:369
  76.6 37.5 %reduce.1 = f32[256,128]{1,0:T(8,128)} custom-call(bf16[2,32,64,256]{3,2,1,0:T(8,128)(2,1)} %get-tuple-element.34.buf_ref), custom_call_target="tpu_custom_call" | custom-call | tf_op jit(solution)/shard_map/reduce/pallas_call | solution.py:470
  114.1 1.5 %slice_bitcast_fusion.4 = f32[128,192]{0,1:T(8,128)} fusion(f32[256,128]{1,0:T(8,128)} %reduce.1), kind=kLoop, calls=%fused_computation.10 | loop fusion | bytes 196608 | tf_op jit(solution)/shard_map/transpose | solution.py:524
  115.7 1.4 %slice_bitcast_fusion.5 = f32[128,64]{0,1:T(8,128)} fusion(f32[256,128]{1,0:T(8,128)} %reduce.1), kind=kLoop, calls=%fused_computation.11 | loop fusion | bytes 65536 | tf_op jit(solution)/shard_map/transpose | solution.py:524
  (4 shorter events, 0.1 us)
Async XLA Ops:
  64.2 1.0 copy-start.1
  64.2 2.1 %copy-start = (f32[2,2,384,512]{3,2,1,0:T(8,128)S(1)}, f32[2,2,384,512]{3,2,1,0:T(8,128)}, u32[]{:S(2)}) copy-start(f32[2,2,384,512]{3,2,1,0:T(8,128)} %get-tuple-element.26) | copy-start | bytes 9437188
